TPU v7x, 256 devices: a whole 4x4x8 slice. The times are simulated.
256 devices in a mesh: head: 8 (over z_lo, y), tok: 32 (over x, z_hi, core).
Axes of the slice: x: 4, y: 4, z: 8 (z_hi: 4, z_lo: 2; z = z_hi * 2 + z_lo), core: 2. Of those that a mesh axis runs over, the one named last changes fastest.
Arguments:
- queries: bfloat16 [2, 16, 8192, 256], P(None, 'head', 'tok'), may hold values from -6 to 6
- key_vectors: bfloat16 [2, 16, 8192, 256], P(None, 'head', 'tok'), may hold values from -6 to 6
- value_vectors: bfloat16 [2, 16, 8192, 256], P(None, 'head', 'tok'), may hold values from -6 to 6
- step_rates: bfloat16 [2, 16, 8192], P(None, 'head', 'tok'), may hold values from 0.029907227 to 0.29882812
- counts: int32 [2, 32], replicated, may hold values from 1 to 256, 5120 in all within a row
- out_gain: float32 [16, 256], P('head'), may hold values from 0.25 to 1.75
- w_gate: float32 [16, 512, 256], P('head', 'tok'), may hold values from -0.375 to 0.375
- w_up: float32 [16, 512, 256], P('head', 'tok'), may hold values from -0.375 to 0.375
- w_down: float32 [16, 256, 512], P('head', 'tok'), may hold values from -0.25 to 0.25
Outputs:
- mixed_out: bfloat16 [2, 16, 8192, 256], P(None, 'head', 'tok')
- final_gate: float32 [16, 512, 256], P('head', 'tok')
- final_up: float32 [16, 512, 256], P('head', 'tok')
- final_down: float32 [16, 256, 512], P('head', 'tok')
Inputs may be any that keep to these rules, and one draw needn't show every extreme that they name: `counts`: the valid tokens are the first ones of each block of 256; each row sums to 256 * 32 * 5 // 8 and some block of each group is full.
All inputs are finite; a program needn't handle non-finite values.
Results may differ from a plain program's by a relative error of at most 0.011.
Values may be sent and summed in bfloat16 or wider, within the bound.
No kernel may reach another device: no remote copies, remote signals or barrier semaphores. Data moves between devices by JAX's collectives and lax.ppermute only.
A program may use at most 64 MiB of HBM per device.

v0:
```python
import functools

import jax
import jax.numpy as jnp
from jax import lax
from jax.experimental import pallas as pl
from jax.experimental.pallas import tpu as pltpu
from jax.sharding import Mesh, PartitionSpec as P

HEADS = 16
DH = 256
FH = 512
BLK = 256
EPS = 1e-06
NX = 4
NZ = 4
ROWS = 96

VMEM = pl.BlockSpec(memory_space=pltpu.VMEM)
SMEM = pl.BlockSpec(memory_space=pltpu.SMEM)
NT = (((1,), (1,)), ((), ()))
NN = (((1,), (0,)), ((), ()))
f32 = jnp.float32
bf16 = jnp.bfloat16


def on_chip(shape, dtype=bf16):
    return pltpu.VMEM(shape, dtype)


def call(kernel, operands, outs, scalars=(), hbm=(), scratch=(), limit=8):
    held = [pltpu.with_memory_space_constraint(v, pltpu.VMEM) for v in operands]
    hbm = [pltpu.with_memory_space_constraint(v, pltpu.HBM) for v in hbm]
    return pl.pallas_call(
        kernel,
        in_specs=[SMEM] * len(scalars) + [VMEM] * (len(held) + len(hbm)),
        out_specs=[VMEM] * len(outs),
        out_shape=list(outs),
        scratch_shapes=list(scratch),
        compiler_params=pltpu.CompilerParams(vmem_limit_bytes=limit << 20),
    )(*scalars, *held, *hbm)


def position():
    return lax.axis_index("tx"), lax.axis_index("tz"), lax.axis_index("core")


def shift(array, axis, d):
    pairs = []
    for i in range(4):
        pairs += [(2 * i, 2 * (i ^ d)), (2 * i + 1, 2 * (i ^ ((4 - d) % 4)) + 1)]
    return lax.ppermute(array, (axis, "core"), pairs)


SWAP = [(0, 1), (1, 0)]


def mm(a, b, dims=NN):
    return lax.dot_general(a, b, dims, preferred_element_type=f32)


def chip_index(dx, dz):
    tx, tz, core = position()
    px = jnp.bitwise_xor(tx, jnp.where(core == 0, dx, (4 - dx) % 4))
    pz = jnp.bitwise_xor(tz, jnp.where(core == 0, dz, (4 - dz) % 4))
    return px * NZ + pz


def assemble(stacks, g_ref, u_ref, d_ref):
    for dx in range(NX):
        for dz in range(NZ):
            p = chip_index(dx, dz)
            f0 = pl.multiple_of(p * 32, 32)
            d0 = pl.multiple_of(p * 16, 16)
            g_ref[pl.ds(f0, 32), :] = stacks[dx][dz, 0:32, :]
            u_ref[pl.ds(f0, 32), :] = stacks[dx][dz, 32:64, :]
            d_ref[pl.ds(d0, 16), 0:256] = stacks[dx][dz, 64:80, :]
            d_ref[pl.ds(d0, 16), 256:512] = stacks[dx][dz, 80:96, :]


def split_kernel(wg, wu, wd, own, send):
    core = position()[2]
    for head, out in ((core, own), (1 - core, send)):
        out[0:16, :] = wg[head]
        out[16:32, :] = wu[head]
        out[32:40, :] = wd[head, :, 0:256]
        out[40:48, :] = wd[head, :, 256:512]


def merge_kernel(own, recv, w, piece):
    first = position()[2] == 0
    mine, theirs = own[...], recv[...]
    low = jnp.where(first, mine, theirs)
    high = jnp.where(first, theirs, mine)
    for row, size, to in ((0, 16, 0), (16, 16, 32), (32, 8, 64), (40, 8, 80)):
        w[to : to + size, :] = low[row : row + size]
        w[to + size : to + 2 * size, :] = high[row : row + size]
    piece[...] = w[...].astype(bf16)


def final_kernel(own, recv, wg, wu, wd):
    core = position()[2]
    for head, rows in ((core, own), (1 - core, recv)):
        wg[head] = rows[0:16, :]
        wu[head] = rows[16:32, :]
        wd[head, :, 0:256] = rows[32:40, :]
        wd[head, :, 256:512] = rows[40:48, :]


def tokens_kernel(counts, queries, keys, values, rates, gain_in, *outs):
    outs[8][...] = gain_in[...]
    ke_own, q_own, ke_out, q_out = outs[0:2], outs[2:4], outs[4:6], outs[6:8]
    tx, tz, core = position()
    tok = (tx * NZ + tz) * 2 + core
    grad_scale = float(2 * NX * NZ * BLK) ** (-0.5)
    lane = lax.broadcasted_iota(jnp.int32, (1, BLK), 1)
    for head, sends in ((core, False), (1 - core, True)):
        for g in range(2):
            valid = (lane < counts[g, tok]).astype(f32)
            both = rates[g].astype(f32)
            row = jnp.where(head == 0, both[0:1], both[1:2]) * grad_scale * valid
            col = jnp.broadcast_to(row, (128, BLK)).T
            col = jnp.concatenate([col, col], axis=1)
            e = (values[g, head].astype(f32) * col).astype(bf16)
            ke, q = (ke_out[g], q_out[g]) if sends else (ke_own[g], q_own[g])
            ke[0], ke[1], q[...] = keys[g, head], e, queries[g, head]


def update_kernel(
    ke, ke_other, s0, s1, s2, s3, own, o1, o2, o3, g_ref, u_ref, d_ref,
    dt_ref, k_ref, e_ref, et_ref, dg_ref, du_ref, dd_ref,
):
    assemble((s0, s1, s2, s3), g_ref, u_ref, d_ref)
    k_ref[0:BLK, :] = ke[0]
    k_ref[BLK:, :] = ke_other[0]
    e_ref[0:BLK, :] = ke[1]
    e_ref[BLK:, :] = ke_other[1]
    dt_ref[...] = d_ref[...].T
    et_ref[...] = e_ref[...].T
    a = mm(g_ref[...], k_ref[...], NT)
    b = mm(u_ref[...], k_ref[...], NT)
    r = mm(dt_ref[...], e_ref[...], NT)
    s = jax.nn.sigmoid(a)
    act = a * s
    hid = (act * b).astype(bf16)
    da = (r * b * s * (1.0 + a * (1.0 - s))).astype(bf16)
    db = (r * act).astype(bf16)
    dg_ref[...] = mm(da, k_ref[...])
    du_ref[...] = mm(db, k_ref[...])
    dd_ref[...] = mm(et_ref[...], hid, NT)
    for dx, out in enumerate((own, o1, o2, o3)):
        for dz in range(NZ):
            p = chip_index(dx, dz)
            f0 = pl.multiple_of(p * 32, 32)
            d0 = pl.multiple_of(p * 16, 16)
            out[dz, 0:32, :] = dg_ref[pl.ds(f0, 32), :].astype(out.dtype)
            out[dz, 32:64, :] = du_ref[pl.ds(f0, 32), :].astype(out.dtype)
            out[dz, 64:80, :] = dd_ref[pl.ds(d0, 16), 0:256].astype(out.dtype)
            out[dz, 80:96, :] = dd_ref[pl.ds(d0, 16), 256:512].astype(out.dtype)


WEIGHTS = (((FH, DH), bf16), ((FH, DH), bf16), ((DH, FH), bf16))


def update(stacks, ke, ke_other, keep):
    weights = [on_chip(*w) for w in WEIGHTS]
    outs = [on_chip((NZ, ROWS, DH), f32)] + [on_chip((NZ, ROWS, DH))] * 3
    scratch = [
        pltpu.VMEM((FH, DH), bf16),
        pltpu.VMEM((2 * BLK, DH), bf16),
        pltpu.VMEM((2 * BLK, DH), bf16),
        pltpu.VMEM((DH, 2 * BLK), bf16),
        pltpu.VMEM((FH, DH), f32),
        pltpu.VMEM((FH, DH), f32),
        pltpu.VMEM((DH, FH), f32),
    ]
    operands = (ke, ke_other, *stacks)
    if keep:
        got = call(update_kernel, operands, outs + weights, scratch=scratch, limit=20)
        return got[:4], got[4:]
    return call(update_kernel, operands, outs, scratch=weights + scratch, limit=20), None


def partial_kernel(own, r1, r2, r3, y0, y1, y2, y3):
    for dz, out in enumerate((y0, y1, y2, y3)):
        total = own[dz] + r1[dz].astype(f32) + r2[dz].astype(f32) + r3[dz].astype(f32)
        out[...] = total.astype(out.dtype)


def partial_sum(own, recv):
    return call(
        partial_kernel, (own, *recv), [on_chip((ROWS, DH), f32)] + [on_chip((ROWS, DH))] * 3
    )


def renorm_kernel(w, y0, t1, t2, t3, piece, *outs, last):
    old = w[...]
    new = old + (y0[...] + t1[...].astype(f32) + t2[...].astype(f32) + t3[...].astype(f32))

    def mean_square(v):
        sums = jnp.sum(v * v, axis=-1, keepdims=True)
        wide = (sums[64:80] + sums[80:96]) * (1.0 / FH)
        return jnp.concatenate([sums[0:64] * (1.0 / DH), wide, wide], axis=0)

    scaled = new * jnp.sqrt(mean_square(old)) * lax.rsqrt(mean_square(new) + EPS)
    piece[...] = scaled.astype(bf16)
    if not last:
        outs[0][...] = scaled
        return
    first = position()[2] == 0
    for row, size, at in ((0, 16, 0), (16, 16, 32), (32, 8, 64), (40, 8, 80)):
        low = scaled[at : at + size, :]
        high = scaled[at + size : at + 2 * size, :]
        outs[0][row : row + size, :] = jnp.where(first, low, high)
        outs[1][row : row + size, :] = jnp.where(first, high, low)


def renorm(w, y0, recv, last=False):
    held = [on_chip((48, DH), f32)] * 2 if last else [on_chip((ROWS, DH), f32)]
    return call(
        functools.partial(renorm_kernel, last=last), (w, y0, *recv), [on_chip((ROWS, DH)), *held]
    )


def apply_kernel(q, q_other, *refs, assembled):
    if assembled:
        g_ref, u_ref, d_ref, o_own, o_send, sq = refs
    else:
        o_own, o_send, sq, g_ref, u_ref, d_ref = refs[4:]
        assemble(refs[:4], g_ref, u_ref, d_ref)
    for which, (query, out) in enumerate(((q, o_own), (q_other, o_send))):
        a = mm(query[...], g_ref[...], NT)
        b = mm(query[...], u_ref[...], NT)
        hid = (a * jax.nn.sigmoid(a) * b).astype(bf16)
        o = mm(hid, d_ref[...], NT)
        out[...] = o.astype(out.dtype)
        sums = jnp.sum(o * o, axis=-1, keepdims=True)
        sq[which] = jnp.broadcast_to(sums, (BLK, 128)).T[0:4, :]


def apply(q, q_other, weights, assembled):
    return call(
        functools.partial(apply_kernel, assembled=assembled),
        (q, q_other, *weights),
        [on_chip((BLK, DH), f32), on_chip((BLK, DH)), on_chip((2, 4, BLK), f32)],
        scratch=() if assembled else [pltpu.VMEM(*w) for w in WEIGHTS],
        limit=16,
    )


def finish_kernel(counts, o0, r0, o1, r1, sq, gain, out):
    tx, tz, core = position()
    tok = (tx * NZ + tz) * 2 + core
    for g, (own, other) in enumerate(((o0, r0), (o1, r1))):
        valid = lax.broadcasted_iota(jnp.int32, (1, BLK), 1) < counts[g, tok]
        row = lax.rsqrt(sq[4 * g : 4 * g + 1, :] * (1.0 / (HEADS * DH)) + EPS)
        scale = jnp.broadcast_to(jnp.where(valid, row, 0.0), (128, BLK)).T
        scale = jnp.concatenate([scale, scale], axis=1)
        for head, o in ((core, own), (1 - core, other)):
            out[g, head] = (o[...].astype(f32) * gain[pl.ds(head, 1), :] * scale).astype(bf16)


def gather_rows(piece):
    parts = [piece] + [shift(piece, "tz", d) for d in (1, 2, 3)]
    stack = jnp.stack(parts)
    return [stack] + [shift(stack, "tx", d) for d in (1, 2, 3)]


def scatter_rows(sends):
    recv = [shift(sends[d], "tx", d) for d in (1, 2, 3)]
    y = partial_sum(sends[0], recv)
    return y[0], [shift(y[d], "tz", d) for d in (1, 2, 3)]


def head_sum(sq):
    sq = sq + sum(shift(sq, "hy", d) for d in (1, 2, 3))
    return sq + lax.ppermute(sq, "hz", SWAP)


def swap(array):
    return lax.ppermute(array, "core", SWAP)


def on_device(
    queries, key_vectors, value_vectors, step_rates, counts, out_gain, w_gate, w_up, w_down
):
    half = on_chip((48, DH), f32)
    own, send = call(split_kernel, (), [half, half], hbm=(w_gate, w_up, w_down))
    masters, piece = call(
        merge_kernel, (own, swap(send)), [on_chip((ROWS, DH), f32), on_chip((ROWS, DH))]
    )
    piece, tokens = lax.optimization_barrier(
        (piece, (queries, key_vectors, value_vectors, step_rates))
    )
    pair, single = on_chip((2, BLK, DH)), on_chip((BLK, DH))
    got = call(
        tokens_kernel,
        (),
        [pair, pair, single, single] * 2 + [on_chip((2, DH), f32)],
        scalars=(counts,),
        hbm=(*tokens, out_gain),
        limit=16,
    )
    ke, q = got[0:2], got[2:4]
    ke_other = [swap(v) for v in got[4:6]]
    q_other = [swap(v) for v in got[6:8]]

    stacks = gather_rows(piece)
    sends, _ = update(stacks, ke[0], ke_other[0], False)
    piece, masters = renorm(masters, *scatter_rows(sends))
    stacks = gather_rows(piece)
    sends, weights = update(stacks, ke[1], ke_other[1], True)
    o0, o0_send, sq0 = apply(q[0], q_other[0], weights, True)
    r0 = swap(o0_send)
    piece, own, send = renorm(masters, *scatter_rows(sends), last=True)
    stacks = gather_rows(piece)
    finals = call(
        final_kernel,
        (own, swap(send)),
        [
            jax.ShapeDtypeStruct((2, 16, DH), f32),
            jax.ShapeDtypeStruct((2, 16, DH), f32),
            jax.ShapeDtypeStruct((2, 8, FH), f32),
        ],
    )
    stacks[0], finals = lax.optimization_barrier((stacks[0], finals))
    o1, o1_send, sq1 = apply(q[1], q_other[1], stacks, False)
    sq = jnp.concatenate([sq0, sq1], axis=1)
    total = head_sum(sq[0] + swap(sq[1]))
    r1 = swap(o1_send)
    (mixed,) = call(
        finish_kernel,
        (o0, r0, o1, r1, total, got[8]),
        [jax.ShapeDtypeStruct((2, 2, BLK, DH), bf16)],
        scalars=(counts,),
    )
    return (mixed, *finals)


def solution(mesh):
    grid = Mesh(mesh.devices.reshape(2, 4, NX, NZ, 2), ("hz", "hy", "tx", "tz", "core"))
    head, tok = ("hz", "hy"), ("tx", "tz", "core")
    tokens = P(None, head, tok, None)
    rows = P(head, tok, None)
    return jax.shard_map(
        on_device,
        mesh=grid,
        in_specs=(tokens, tokens, tokens, P(None, head, tok), P(), P(head, None), rows, rows, rows),
        out_specs=(tokens, rows, rows, rows),
        check_vma=False,
    )
```

profile of v0, /device:TPU:32, one launch (start us, length us, event | category | flops | bytes accessed | tf_op | source)
XLA Modules:
  0.0 142.6 jit_solution(16209347810103661868)
XLA Ops:
  0.6 0.8 shard_map.120
  1.5 1.2 collective-permute-done.recv
  2.8 5.5 %collective-permute-start.6 = (bf16[96,256]{1,0:T(8,128)(2,1)S(1)}, bf16[96,256]{1,0:T(8,128)(2,1)S(1)}, u32[]{:S(2)}, u32[]{:S(2)}) collective-permute-start(bf16[96,256]{1,0:T(8,128)(2,1)S(1)} %get-tuple-element.73), channel_id=1, source_target_pairs={{0,6},{1,3},{2,4},{3,1},{4,2},{5,7},{6,0},{7,5},{8,14},{9,11},{10,... | collective-permute-start | bytes 147464 | tf_op jit(solution)/shard_map/ppermute | solution.py:52
  8.3 1.4 %collective-permute-start.5 = (bf16[96,256]{1,0:T(8,128)(2,1)S(1)}, bf16[96,256]{1,0:T(8,128)(2,1)S(1)}, u32[]{:S(2)}, u32[]{:S(2)}) collective-permute-start(bf16[96,256]{1,0:T(8,128)(2,1)S(1)} %get-tuple-element.73), channel_id=1, source_target_pairs={{0,4},{1,5},{2,6},{3,7},{4,0},{5,1},{6,2},{7,3},{8,12},{9,13},{10,... | collective-permute-start | bytes 147464 | tf_op jit(solution)/shard_map/ppermute | solution.py:52
  9.7 1.0 collective-permute-start.4
  10.7 1.6 %shard_map.122 = (bf16[2,256,256]{2,1,0:T(8,128)(2,1)S(1)}, bf16[2,256,256]{2,1,0:T(8,128)(2,1)S(1)}, bf16[256,256]{1,0:T(8,128)(2,1)S(1)}, bf16[256,256]{1,0:T(...) custom-call(s32[2,32]{1,0:T(2,128)S(1)} %copy-done, ...), custom_call_target="tpu_custom_call" | custom-call | tf_op jit(solution)/shard_map/pallas_call | solution.py:34
  12.5 4.3 %collective-permute-done.5 = bf16[96,256]{1,0:T(8,128)(2,1)S(1)} collective-permute-done((bf16[96,256]{1,0:T(8,128)(2,1)S(1)}, bf16[96,256]{1,0:T(8,128)(2,1)S(1)}, u32[]{:S(2)}, u32[]{:S(2)}) %collective-permute-start.5) | collective-permute-done | bytes 49184 | tf_op jit(solution)/shard_map/ppermute | solution.py:52
  16.8 2.8 %collective-permute-start.9 = (bf16[4,96,256]{2,1,0:T(8,128)(2,1)S(1)}, bf16[4,96,256]{2,1,0:T(8,128)(2,1)S(1)}, u32[]{:S(2)}, u32[]{:S(2)}) collective-permute-start(bf16[4,96,256]{2,1,0:T(8,128)(2,1)S(1)} %pad_maximum_fusion.s0), channel_id=1, source_target_pairs={{0,24},{1,9},{8,16},{9,1},{16,8},{17,25},{24,0},{25,17},{2,26},{3,... | collective-permute-start | bytes 589832 | tf_op jit(solution)/shard_map/ppermute | solution.py:52
  19.7 0.8 collective-permute-start.8
  20.5 0.5 collective-permute-start.7
  21.0 7.9 %collective-permute-done.9.s3 = bf16[4,96,256]{2,1,0:T(8,128)(2,1)S(1)} collective-permute-done((bf16[4,96,256]{2,1,0:T(8,128)(2,1)S(1)}, bf16[4,96,256]{2,1,0:T(8,128)(2,1)S(1)}, u32[]{:S(2)}, u32[]{:S(2)}) %collective-permute-start.9) | collective-permute-done | bytes 196640 | tf_op jit(solution)/shard_map/ppermute | solution.py:52
  28.9 1.3 shard_map.123
  30.2 0.9 collective-permute-start.10
  31.1 4.4 %collective-permute-start.11 = (bf16[4,96,256]{2,1,0:T(8,128)(2,1)S(1)}, bf16[4,96,256]{2,1,0:T(8,128)(2,1)S(1)}, u32[]{:S(2)}, u32[]{:S(2)}) collective-permute-start(bf16[4,96,256]{2,1,0:T(8,128)(2,1)S(1)} %get-tuple-element.76), channel_id=1, source_target_pairs={{0,16},{1,17},{8,24},{9,25},{16,0},{17,1},{24,8},{25,9},{2,18},{3,... | collective-permute-start | bytes 589832 | tf_op jit(solution)/shard_map/ppermute | solution.py:52
  35.5 0.7 collective-permute-done.10.r1
  36.2 8.3 %collective-permute-done.11.r2 = bf16[4,96,256]{2,1,0:T(8,128)(2,1)S(1)} collective-permute-done((bf16[4,96,256]{2,1,0:T(8,128)(2,1)S(1)}, bf16[4,96,256]{2,1,0:T(8,128)(2,1)S(1)}, u32[]{:S(2)}, u32[]{:S(2)}) %collective-permute-start.11) | collective-permute-done | bytes 196640 | tf_op jit(solution)/shard_map/ppermute | solution.py:52
  44.5 0.9 collective-permute-done.12.r3
  45.5 0.9 collective-permute-start.13
  46.4 2.9 %collective-permute-start.14 = (bf16[96,256]{1,0:T(8,128)(2,1)S(1)}, bf16[96,256]{1,0:T(8,128)(2,1)S(1)}, u32[]{:S(2)}, u32[]{:S(2)}) collective-permute-start(bf16[96,256]{1,0:T(8,128)(2,1)S(1)} %get-tuple-element.80), channel_id=1, source_target_pairs={{0,4},{1,5},{2,6},{3,7},{4,0},{5,1},{6,2},{7,3},{8,12},{9,13},{10,... | collective-permute-start | bytes 147464 | tf_op jit(solution)/shard_map/ppermute | solution.py:52
  49.3 2.8 %collective-permute-start.15 = (bf16[96,256]{1,0:T(8,128)(2,1)S(1)}, bf16[96,256]{1,0:T(8,128)(2,1)S(1)}, u32[]{:S(2)}, u32[]{:S(2)}) collective-permute-start(bf16[96,256]{1,0:T(8,128)(2,1)S(1)} %get-tuple-element.81), channel_id=1, source_target_pairs={{0,6},{1,3},{2,4},{3,1},{4,2},{5,7},{6,0},{7,5},{8,14},{9,11},{10,... | collective-permute-start | bytes 147464 | tf_op jit(solution)/shard_map/ppermute | solution.py:52
  52.1 2.5 %collective-permute-done.14.t2 = bf16[96,256]{1,0:T(8,128)(2,1)S(1)} collective-permute-done((bf16[96,256]{1,0:T(8,128)(2,1)S(1)}, bf16[96,256]{1,0:T(8,128)(2,1)S(1)}, u32[]{:S(2)}, u32[]{:S(2)}) %collective-permute-start.14) | collective-permute-done | bytes 49184 | tf_op jit(solution)/shard_map/ppermute | solution.py:52
  54.6 1.9 %collective-permute-done.15.t3 = bf16[96,256]{1,0:T(8,128)(2,1)S(1)} collective-permute-done((bf16[96,256]{1,0:T(8,128)(2,1)S(1)}, bf16[96,256]{1,0:T(8,128)(2,1)S(1)}, u32[]{:S(2)}, u32[]{:S(2)}) %collective-permute-start.15) | collective-permute-done | bytes 49184 | tf_op jit(solution)/shard_map/ppermute | solution.py:52
  56.8 1.8 %collective-permute-start.18 = (bf16[96,256]{1,0:T(8,128)(2,1)S(1)}, bf16[96,256]{1,0:T(8,128)(2,1)S(1)}, u32[]{:S(2)}, u32[]{:S(2)}) collective-permute-start(bf16[96,256]{1,0:T(8,128)(2,1)S(1)} %get-tuple-element.82), channel_id=1, source_target_pairs={{0,6},{1,3},{2,4},{3,1},{4,2},{5,7},{6,0},{7,5},{8,14},{9,11},{10,... | collective-permute-start | bytes 147464 | tf_op jit(solution)/shard_map/ppermute | solution.py:52
  58.6 2.9 %collective-permute-start.17 = (bf16[96,256]{1,0:T(8,128)(2,1)S(1)}, bf16[96,256]{1,0:T(8,128)(2,1)S(1)}, u32[]{:S(2)}, u32[]{:S(2)}) collective-permute-start(bf16[96,256]{1,0:T(8,128)(2,1)S(1)} %get-tuple-element.82), channel_id=1, source_target_pairs={{0,4},{1,5},{2,6},{3,7},{4,0},{5,1},{6,2},{7,3},{8,12},{9,13},{10,... | collective-permute-start | bytes 147464 | tf_op jit(solution)/shard_map/ppermute | solution.py:52
  61.4 1.9 %collective-permute-start.16 = (bf16[96,256]{1,0:T(8,128)(2,1)S(1)}, bf16[96,256]{1,0:T(8,128)(2,1)S(1)}, u32[]{:S(2)}, u32[]{:S(2)}) collective-permute-start(bf16[96,256]{1,0:T(8,128)(2,1)S(1)} %get-tuple-element.82), channel_id=1, source_target_pairs={{0,2},{1,7},{2,0},{3,5},{4,6},{5,3},{6,4},{7,1},{8,10},{9,15},{10,... | collective-permute-start | bytes 147464 | tf_op jit(solution)/shard_map/ppermute | solution.py:52
  63.4 3.7 %collective-permute-done.17 = bf16[96,256]{1,0:T(8,128)(2,1)S(1)} collective-permute-done((bf16[96,256]{1,0:T(8,128)(2,1)S(1)}, bf16[96,256]{1,0:T(8,128)(2,1)S(1)}, u32[]{:S(2)}, u32[]{:S(2)}) %collective-permute-start.17) | collective-permute-done | bytes 49184 | tf_op jit(solution)/shard_map/ppermute | solution.py:52
  67.1 1.8 %collective-permute-start.21 = (bf16[4,96,256]{2,1,0:T(8,128)(2,1)S(1)}, bf16[4,96,256]{2,1,0:T(8,128)(2,1)S(1)}, u32[]{:S(2)}, u32[]{:S(2)}) collective-permute-start(bf16[4,96,256]{2,1,0:T(8,128)(2,1)S(1)} %pad_maximum_fusion.1.s0), channel_id=1, source_target_pairs={{0,24},{1,9},{8,16},{9,1},{16,8},{17,25},{24,0},{25,17},{2,26},{3,... | collective-permute-start | bytes 589832 | tf_op jit(solution)/shard_map/ppermute | solution.py:52
  69.0 2.5 %collective-permute-start.19 = (bf16[4,96,256]{2,1,0:T(8,128)(2,1)S(1)}, bf16[4,96,256]{2,1,0:T(8,128)(2,1)S(1)}, u32[]{:S(2)}, u32[]{:S(2)}) collective-permute-start(bf16[4,96,256]{2,1,0:T(8,128)(2,1)S(1)} %pad_maximum_fusion.1.s0), channel_id=1, source_target_pairs={{0,8},{1,25},{8,0},{9,17},{16,24},{17,9},{24,16},{25,1},{2,10},{3,... | collective-permute-start | bytes 589832 | tf_op jit(solution)/shard_map/ppermute | solution.py:52
  71.5 7.5 %collective-permute-done.21.s3 = bf16[4,96,256]{2,1,0:T(8,128)(2,1)S(1)} collective-permute-done((bf16[4,96,256]{2,1,0:T(8,128)(2,1)S(1)}, bf16[4,96,256]{2,1,0:T(8,128)(2,1)S(1)}, u32[]{:S(2)}, u32[]{:S(2)}) %collective-permute-start.21) | collective-permute-done | bytes 196640 | tf_op jit(solution)/shard_map/ppermute | solution.py:52
  79.1 1.3 shard_map.126
  80.5 2.4 %collective-permute-start.25 = (bf16[4,96,256]{2,1,0:T(8,128)(2,1)S(1)}, bf16[4,96,256]{2,1,0:T(8,128)(2,1)S(1)}, u32[]{:S(2)}, u32[]{:S(2)}) collective-permute-start(bf16[4,96,256]{2,1,0:T(8,128)(2,1)S(1)} %get-tuple-element.93), channel_id=1, source_target_pairs={{0,16},{1,17},{8,24},{9,25},{16,0},{17,1},{24,8},{25,9},{2,18},{3,... | collective-permute-start | bytes 589832 | tf_op jit(solution)/shard_map/ppermute | solution.py:52
  82.9 2.3 %collective-permute-start.26 = (bf16[4,96,256]{2,1,0:T(8,128)(2,1)S(1)}, bf16[4,96,256]{2,1,0:T(8,128)(2,1)S(1)}, u32[]{:S(2)}, u32[]{:S(2)}) collective-permute-start(bf16[4,96,256]{2,1,0:T(8,128)(2,1)S(1)} %get-tuple-element.94), channel_id=1, source_target_pairs={{0,24},{1,9},{8,16},{9,1},{16,8},{17,25},{24,0},{25,17},{2,26},{3,... | collective-permute-start | bytes 589832 | tf_op jit(solution)/shard_map/ppermute | solution.py:52
  85.2 2.2 %collective-permute-done.24.r1 = bf16[4,96,256]{2,1,0:T(8,128)(2,1)S(1)} collective-permute-done((bf16[4,96,256]{2,1,0:T(8,128)(2,1)S(1)}, bf16[4,96,256]{2,1,0:T(8,128)(2,1)S(1)}, u32[]{:S(2)}, u32[]{:S(2)}) %collective-permute-start.24) | collective-permute-done | bytes 196640 | tf_op jit(solution)/shard_map/ppermute | solution.py:52
  87.4 4.6 %collective-permute-done.25.r2 = bf16[4,96,256]{2,1,0:T(8,128)(2,1)S(1)} collective-permute-done((bf16[4,96,256]{2,1,0:T(8,128)(2,1)S(1)}, bf16[4,96,256]{2,1,0:T(8,128)(2,1)S(1)}, u32[]{:S(2)}, u32[]{:S(2)}) %collective-permute-start.25) | collective-permute-done | bytes 196640 | tf_op jit(solution)/shard_map/ppermute | solution.py:52
  92.0 0.7 collective-permute-done.26.r3
  92.8 1.1 collective-permute-start.27
  93.9 3.1 %collective-permute-start.28 = (bf16[96,256]{1,0:T(8,128)(2,1)S(1)}, bf16[96,256]{1,0:T(8,128)(2,1)S(1)}, u32[]{:S(2)}, u32[]{:S(2)}) collective-permute-start(bf16[96,256]{1,0:T(8,128)(2,1)S(1)} %get-tuple-element.97), channel_id=1, source_target_pairs={{0,4},{1,5},{2,6},{3,7},{4,0},{5,1},{6,2},{7,3},{8,12},{9,13},{10,... | collective-permute-start | bytes 147464 | tf_op jit(solution)/shard_map/ppermute | solution.py:52
  97.0 2.4 %collective-permute-start.29 = (bf16[96,256]{1,0:T(8,128)(2,1)S(1)}, bf16[96,256]{1,0:T(8,128)(2,1)S(1)}, u32[]{:S(2)}, u32[]{:S(2)}) collective-permute-start(bf16[96,256]{1,0:T(8,128)(2,1)S(1)} %get-tuple-element.98), channel_id=1, source_target_pairs={{0,6},{1,3},{2,4},{3,1},{4,2},{5,7},{6,0},{7,5},{8,14},{9,11},{10,... | collective-permute-start | bytes 147464 | tf_op jit(solution)/shard_map/ppermute | solution.py:52
  99.4 2.7 %collective-permute-done.28.t2 = bf16[96,256]{1,0:T(8,128)(2,1)S(1)} collective-permute-done((bf16[96,256]{1,0:T(8,128)(2,1)S(1)}, bf16[96,256]{1,0:T(8,128)(2,1)S(1)}, u32[]{:S(2)}, u32[]{:S(2)}) %collective-permute-start.28) | collective-permute-done | bytes 49184 | tf_op jit(solution)/shard_map/ppermute | solution.py:52
  102.1 1.1 collective-permute-done.29.t3
  103.3 0.2 shard_map.129
  103.5 2.8 %collective-permute-start.32 = (bf16[96,256]{1,0:T(8,128)(2,1)S(1)}, bf16[96,256]{1,0:T(8,128)(2,1)S(1)}, u32[]{:S(2)}, u32[]{:S(2)}) collective-permute-start(bf16[96,256]{1,0:T(8,128)(2,1)S(1)} %get-tuple-element.99), channel_id=1, source_target_pairs={{0,6},{1,3},{2,4},{3,1},{4,2},{5,7},{6,0},{7,5},{8,14},{9,11},{10,... | collective-permute-start | bytes 147464 | tf_op jit(solution)/shard_map/ppermute | solution.py:52
  106.3 2.8 %collective-permute-start.31 = (bf16[96,256]{1,0:T(8,128)(2,1)S(1)}, bf16[96,256]{1,0:T(8,128)(2,1)S(1)}, u32[]{:S(2)}, u32[]{:S(2)}) collective-permute-start(bf16[96,256]{1,0:T(8,128)(2,1)S(1)} %get-tuple-element.99), channel_id=1, source_target_pairs={{0,4},{1,5},{2,6},{3,7},{4,0},{5,1},{6,2},{7,3},{8,12},{9,13},{10,... | collective-permute-start | bytes 147464 | tf_op jit(solution)/shard_map/ppermute | solution.py:52
  109.1 1.0 collective-permute-start.30
  110.1 4.2 %collective-permute-done.31 = bf16[96,256]{1,0:T(8,128)(2,1)S(1)} collective-permute-done((bf16[96,256]{1,0:T(8,128)(2,1)S(1)}, bf16[96,256]{1,0:T(8,128)(2,1)S(1)}, u32[]{:S(2)}, u32[]{:S(2)}) %collective-permute-start.31) | collective-permute-done | bytes 49184 | tf_op jit(solution)/shard_map/ppermute | solution.py:52
  114.3 0.3 collective-permute-done.30
  114.7 2.1 %collective-permute-start.36 = (bf16[4,96,256]{2,1,0:T(8,128)(2,1)S(1)}, bf16[4,96,256]{2,1,0:T(8,128)(2,1)S(1)}, u32[]{:S(2)}, u32[]{:S(2)}) collective-permute-start(bf16[4,96,256]{2,1,0:T(8,128)(2,1)S(1)} %pad_maximum_fusion.2.refs_0_), channel_id=1, source_target_pairs={{0,24},{1,9},{8,16},{9,1},{16,8},{17,25},{24,0},{25,17},{2,26},{3,... | collective-permute-start | bytes 589832 | tf_op jit(solution)/shard_map/ppermute | solution.py:52
  116.8 2.1 %collective-permute-start.34 = (bf16[4,96,256]{2,1,0:T(8,128)(2,1)S(1)}, bf16[4,96,256]{2,1,0:T(8,128)(2,1)S(1)}, u32[]{:S(2)}, u32[]{:S(2)}) collective-permute-start(bf16[4,96,256]{2,1,0:T(8,128)(2,1)S(1)} %pad_maximum_fusion.2.refs_0_), channel_id=1, source_target_pairs={{0,8},{1,25},{8,0},{9,17},{16,24},{17,9},{24,16},{25,1},{2,10},{3,... | collective-permute-start | bytes 589832 | tf_op jit(solution)/shard_map/ppermute | solution.py:52
  118.8 0.5 collective-permute-start.23
  119.4 0.8 collective-permute-done.1.q_other
  120.3 0.9 shard_map.127
  121.4 0.6 shard_map.130
  122.1 4.7 %collective-permute-done.36.refs_3_ = bf16[4,96,256]{2,1,0:T(8,128)(2,1)S(1)} collective-permute-done((bf16[4,96,256]{2,1,0:T(8,128)(2,1)S(1)}, bf16[4,96,256]{2,1,0:T(8,128)(2,1)S(1)}, u32[]{:S(2)}, u32[]{:S(2)}) %collective-permute-start.36) | collective-permute-done | bytes 196640 | tf_op jit(solution)/shard_map/ppermute | solution.py:52
  126.8 0.9 shard_map.131
  127.7 0.3 collective-permute-start.38
  128.1 1.1 collective-permute-done.38
  129.2 3.0 %collective-permute-start.41 = (f32[8,256]{1,0:T(8,128)S(1)}, f32[8,256]{1,0:T(8,128)S(1)}, u32[]{:S(2)}, u32[]{:S(2)}) collective-permute-start(f32[8,256]{1,0:T(8,128)S(1)} %fusion.2), channel_id=1, source_target_pairs={{0,96},{1,33},{32,64},{33,1},{64,32},{65,97},{96,0},{97,65},{2,98}... | collective-permute-start | bytes 24584 | tf_op jit(solution)/shard_map/ppermute | solution.py:52
  132.2 0.6 collective-permute-start.40
  132.8 0.6 collective-permute-start.39
  133.4 0.5 collective-permute-start.37
  133.9 0.3 collective-permute-done.41
  134.2 3.2 %collective-permute-done.40 = f32[8,256]{1,0:T(8,128)S(1)} collective-permute-done((f32[8,256]{1,0:T(8,128)S(1)}, f32[8,256]{1,0:T(8,128)S(1)}, u32[]{:S(2)}, u32[]{:S(2)}) %collective-permute-start.40) | collective-permute-done | bytes 8224 | tf_op jit(solution)/shard_map/ppermute | solution.py:52
  137.5 3.6 %collective-permute-done.42 = f32[8,256]{1,0:T(8,128)S(1)} collective-permute-done((f32[8,256]{1,0:T(8,128)S(1)}, f32[8,256]{1,0:T(8,128)S(1)}, u32[]{:S(2)}, u32[]{:S(2)}) %collective-permute-start.42) | collective-permute-done | bytes 8224 | tf_op jit(solution)/shard_map/ppermute | solution.py:277
  141.1 1.5 %shard_map.132 = bf16[2,2,256,256]{3,2,1,0:T(8,128)(2,1)} custom-call(s32[2,32]{1,0:T(2,128)S(1)} %copy-done, f32[256,256]{1,0:T(8,128)S(1)} %get-tuple-element.86.o0, bf16[256,256]{1,0:T(8,128)(2,1)S(1)} %collective-permute-done.22.r0, f32[256,256]{1,0:T(8,128)S(1)} %get-tuple-element.106.o1, bf16[256,256]{1,0:T(8,128)(2,1)S(1)} %collective-permute-done.37.r1, ...), custom_call_target="tpu_custom_call" | custom-call | tf_op jit(solution)/shard_map/pallas_call | solution.py:34
  (44 shorter events, 1.4 us)
Async XLA Ops:
  1.4 1.3 collective-permute-start
  2.8 8.0 %copy-start = (s32[2,32]{1,0:T(2,128)S(1)}, s32[2,32]{1,0:T(2,128)}, u32[]{:S(2)}) copy-start(s32[2,32]{1,0:T(2,128)} %counts.3) | copy-start | bytes 772
  2.8 9.7 %collective-permute-start.6 = (bf16[96,256]{1,0:T(8,128)(2,1)S(1)}, bf16[96,256]{1,0:T(8,128)(2,1)S(1)}, u32[]{:S(2)}, u32[]{:S(2)}) collective-permute-start(bf16[96,256]{1,0:T(8,128)(2,1)S(1)} %get-tuple-element.73), channel_id=1, source_target_pairs={{0,6},{1,3},{2,4},{3,1},{4,2},{5,7},{6,0},{7,5},{8,14},{9,11},{10,... | collective-permute-start | bytes 147464 | tf_op jit(solution)/shard_map/ppermute | solution.py:52
  8.3 8.5 %collective-permute-start.5 = (bf16[96,256]{1,0:T(8,128)(2,1)S(1)}, bf16[96,256]{1,0:T(8,128)(2,1)S(1)}, u32[]{:S(2)}, u32[]{:S(2)}) collective-permute-start(bf16[96,256]{1,0:T(8,128)(2,1)S(1)} %get-tuple-element.73), channel_id=1, source_target_pairs={{0,4},{1,5},{2,6},{3,7},{4,0},{5,1},{6,2},{7,3},{8,12},{9,13},{10,... | collective-permute-start | bytes 147464 | tf_op jit(solution)/shard_map/ppermute | solution.py:52
  9.7 7.1 %collective-permute-start.4 = (bf16[96,256]{1,0:T(8,128)(2,1)S(1)}, bf16[96,256]{1,0:T(8,128)(2,1)S(1)}, u32[]{:S(2)}, u32[]{:S(2)}) collective-permute-start(bf16[96,256]{1,0:T(8,128)(2,1)S(1)} %get-tuple-element.73), channel_id=1, source_target_pairs={{0,2},{1,7},{2,0},{3,5},{4,6},{5,3},{6,4},{7,1},{8,10},{9,15},{10,... | collective-permute-start | bytes 147464 | tf_op jit(solution)/shard_map/ppermute | solution.py:52
  12.3 16.6 %collective-permute-start.3 = (bf16[2,256,256]{2,1,0:T(8,128)(2,1)S(1)}, bf16[2,256,256]{2,1,0:T(8,128)(2,1)S(1)}, u32[]{:S(2)}, u32[]{:S(2)}) collective-permute-start(bf16[2,256,256]{2,1,0:T(8,128)(2,1)S(1)} %get-tuple-element.72), channel_id=1, source_target_pairs={{0,1},{1,0},{2,3},{3,2},{4,5},{5,4},{6,7},{7,6},{8,9},{9,8},{10,11... | collective-permute-start | bytes 786440 | tf_op jit(solution)/shard_map/ppermute | solution.py:281
  16.8 12.1 %collective-permute-start.9 = (bf16[4,96,256]{2,1,0:T(8,128)(2,1)S(1)}, bf16[4,96,256]{2,1,0:T(8,128)(2,1)S(1)}, u32[]{:S(2)}, u32[]{:S(2)}) collective-permute-start(bf16[4,96,256]{2,1,0:T(8,128)(2,1)S(1)} %pad_maximum_fusion.s0), channel_id=1, source_target_pairs={{0,24},{1,9},{8,16},{9,1},{16,8},{17,25},{24,0},{25,17},{2,26},{3,... | collective-permute-start | bytes 589832 | tf_op jit(solution)/shard_map/ppermute | solution.py:52
  19.7 9.2 %collective-permute-start.8 = (bf16[4,96,256]{2,1,0:T(8,128)(2,1)S(1)}, bf16[4,96,256]{2,1,0:T(8,128)(2,1)S(1)}, u32[]{:S(2)}, u32[]{:S(2)}) collective-permute-start(bf16[4,96,256]{2,1,0:T(8,128)(2,1)S(1)} %pad_maximum_fusion.s0), channel_id=1, source_target_pairs={{0,16},{1,17},{8,24},{9,25},{16,0},{17,1},{24,8},{25,9},{2,18},{3,... | collective-permute-start | bytes 589832 | tf_op jit(solution)/shard_map/ppermute | solution.py:52
  20.5 8.4 %collective-permute-start.7 = (bf16[4,96,256]{2,1,0:T(8,128)(2,1)S(1)}, bf16[4,96,256]{2,1,0:T(8,128)(2,1)S(1)}, u32[]{:S(2)}, u32[]{:S(2)}) collective-permute-start(bf16[4,96,256]{2,1,0:T(8,128)(2,1)S(1)} %pad_maximum_fusion.s0), channel_id=1, source_target_pairs={{0,8},{1,25},{8,0},{9,17},{16,24},{17,9},{24,16},{25,1},{2,10},{3,... | collective-permute-start | bytes 589832 | tf_op jit(solution)/shard_map/ppermute | solution.py:52
  30.2 6.0 %collective-permute-start.10 = (bf16[4,96,256]{2,1,0:T(8,128)(2,1)S(1)}, bf16[4,96,256]{2,1,0:T(8,128)(2,1)S(1)}, u32[]{:S(2)}, u32[]{:S(2)}) collective-permute-start(bf16[4,96,256]{2,1,0:T(8,128)(2,1)S(1)} %get-tuple-element.75), channel_id=1, source_target_pairs={{0,8},{1,25},{8,0},{9,17},{16,24},{17,9},{24,16},{25,1},{2,10},{3,... | collective-permute-start | bytes 589832 | tf_op jit(solution)/shard_map/ppermute | solution.py:52
  31.1 13.5 %collective-permute-start.11 = (bf16[4,96,256]{2,1,0:T(8,128)(2,1)S(1)}, bf16[4,96,256]{2,1,0:T(8,128)(2,1)S(1)}, u32[]{:S(2)}, u32[]{:S(2)}) collective-permute-start(bf16[4,96,256]{2,1,0:T(8,128)(2,1)S(1)} %get-tuple-element.76), channel_id=1, source_target_pairs={{0,16},{1,17},{8,24},{9,25},{16,0},{17,1},{24,8},{25,9},{2,18},{3,... | collective-permute-start | bytes 589832 | tf_op jit(solution)/shard_map/ppermute | solution.py:52
  35.5 9.9 %collective-permute-start.12 = (bf16[4,96,256]{2,1,0:T(8,128)(2,1)S(1)}, bf16[4,96,256]{2,1,0:T(8,128)(2,1)S(1)}, u32[]{:S(2)}, u32[]{:S(2)}) collective-permute-start(bf16[4,96,256]{2,1,0:T(8,128)(2,1)S(1)} %get-tuple-element.77), channel_id=1, source_target_pairs={{0,24},{1,9},{8,16},{9,1},{16,8},{17,25},{24,0},{25,17},{2,26},{3,... | collective-permute-start | bytes 589832 | tf_op jit(solution)/shard_map/ppermute | solution.py:52
  45.5 6.6 %collective-permute-start.13 = (bf16[96,256]{1,0:T(8,128)(2,1)S(1)}, bf16[96,256]{1,0:T(8,128)(2,1)S(1)}, u32[]{:S(2)}, u32[]{:S(2)}) collective-permute-start(bf16[96,256]{1,0:T(8,128)(2,1)S(1)} %get-tuple-element.79), channel_id=1, source_target_pairs={{0,2},{1,7},{2,0},{3,5},{4,6},{5,3},{6,4},{7,1},{8,10},{9,15},{10,... | collective-permute-start | bytes 147464 | tf_op jit(solution)/shard_map/ppermute | solution.py:52
  46.4 8.2 %collective-permute-start.14 = (bf16[96,256]{1,0:T(8,128)(2,1)S(1)}, bf16[96,256]{1,0:T(8,128)(2,1)S(1)}, u32[]{:S(2)}, u32[]{:S(2)}) collective-permute-start(bf16[96,256]{1,0:T(8,128)(2,1)S(1)} %get-tuple-element.80), channel_id=1, source_target_pairs={{0,4},{1,5},{2,6},{3,7},{4,0},{5,1},{6,2},{7,3},{8,12},{9,13},{10,... | collective-permute-start | bytes 147464 | tf_op jit(solution)/shard_map/ppermute | solution.py:52
  49.3 7.3 %collective-permute-start.15 = (bf16[96,256]{1,0:T(8,128)(2,1)S(1)}, bf16[96,256]{1,0:T(8,128)(2,1)S(1)}, u32[]{:S(2)}, u32[]{:S(2)}) collective-permute-start(bf16[96,256]{1,0:T(8,128)(2,1)S(1)} %get-tuple-element.81), channel_id=1, source_target_pairs={{0,6},{1,3},{2,4},{3,1},{4,2},{5,7},{6,0},{7,5},{8,14},{9,11},{10,... | collective-permute-start | bytes 147464 | tf_op jit(solution)/shard_map/ppermute | solution.py:52
  56.8 6.6 %collective-permute-start.18 = (bf16[96,256]{1,0:T(8,128)(2,1)S(1)}, bf16[96,256]{1,0:T(8,128)(2,1)S(1)}, u32[]{:S(2)}, u32[]{:S(2)}) collective-permute-start(bf16[96,256]{1,0:T(8,128)(2,1)S(1)} %get-tuple-element.82), channel_id=1, source_target_pairs={{0,6},{1,3},{2,4},{3,1},{4,2},{5,7},{6,0},{7,5},{8,14},{9,11},{10,... | collective-permute-start | bytes 147464 | tf_op jit(solution)/shard_map/ppermute | solution.py:52
  58.6 8.5 %collective-permute-start.17 = (bf16[96,256]{1,0:T(8,128)(2,1)S(1)}, bf16[96,256]{1,0:T(8,128)(2,1)S(1)}, u32[]{:S(2)}, u32[]{:S(2)}) collective-permute-start(bf16[96,256]{1,0:T(8,128)(2,1)S(1)} %get-tuple-element.82), channel_id=1, source_target_pairs={{0,4},{1,5},{2,6},{3,7},{4,0},{5,1},{6,2},{7,3},{8,12},{9,13},{10,... | collective-permute-start | bytes 147464 | tf_op jit(solution)/shard_map/ppermute | solution.py:52
  61.4 5.7 %collective-permute-start.16 = (bf16[96,256]{1,0:T(8,128)(2,1)S(1)}, bf16[96,256]{1,0:T(8,128)(2,1)S(1)}, u32[]{:S(2)}, u32[]{:S(2)}) collective-permute-start(bf16[96,256]{1,0:T(8,128)(2,1)S(1)} %get-tuple-element.82), channel_id=1, source_target_pairs={{0,2},{1,7},{2,0},{3,5},{4,6},{5,3},{6,4},{7,1},{8,10},{9,15},{10,... | collective-permute-start | bytes 147464 | tf_op jit(solution)/shard_map/ppermute | solution.py:52
  63.3 8.2 %collective-permute-start.2 = (bf16[2,256,256]{2,1,0:T(8,128)(2,1)S(1)}, bf16[2,256,256]{2,1,0:T(8,128)(2,1)S(1)}, u32[]{:S(2)}, u32[]{:S(2)}) collective-permute-start(bf16[2,256,256]{2,1,0:T(8,128)(2,1)S(1)} %get-tuple-element.69), channel_id=1, source_target_pairs={{0,1},{1,0},{2,3},{3,2},{4,5},{5,4},{6,7},{7,6},{8,9},{9,8},{10,11... | collective-permute-start | bytes 786440 | tf_op jit(solution)/shard_map/ppermute | solution.py:281
  67.1 11.9 %collective-permute-start.21 = (bf16[4,96,256]{2,1,0:T(8,128)(2,1)S(1)}, bf16[4,96,256]{2,1,0:T(8,128)(2,1)S(1)}, u32[]{:S(2)}, u32[]{:S(2)}) collective-permute-start(bf16[4,96,256]{2,1,0:T(8,128)(2,1)S(1)} %pad_maximum_fusion.1.s0), channel_id=1, source_target_pairs={{0,24},{1,9},{8,16},{9,1},{16,8},{17,25},{24,0},{25,17},{2,26},{3,... | collective-permute-start | bytes 589832 | tf_op jit(solution)/shard_map/ppermute | solution.py:52
  69.0 10.1 %collective-permute-start.20 = (bf16[4,96,256]{2,1,0:T(8,128)(2,1)S(1)}, bf16[4,96,256]{2,1,0:T(8,128)(2,1)S(1)}, u32[]{:S(2)}, u32[]{:S(2)}) collective-permute-start(bf16[4,96,256]{2,1,0:T(8,128)(2,1)S(1)} %pad_maximum_fusion.1.s0), channel_id=1, source_target_pairs={{0,16},{1,17},{8,24},{9,25},{16,0},{17,1},{24,8},{25,9},{2,18},{3,... | collective-permute-start | bytes 589832 | tf_op jit(solution)/shard_map/ppermute | solution.py:52
  69.0 10.1 %collective-permute-start.19 = (bf16[4,96,256]{2,1,0:T(8,128)(2,1)S(1)}, bf16[4,96,256]{2,1,0:T(8,128)(2,1)S(1)}, u32[]{:S(2)}, u32[]{:S(2)}) collective-permute-start(bf16[4,96,256]{2,1,0:T(8,128)(2,1)S(1)} %pad_maximum_fusion.1.s0), channel_id=1, source_target_pairs={{0,8},{1,25},{8,0},{9,17},{16,24},{17,9},{24,16},{25,1},{2,10},{3,... | collective-permute-start | bytes 589832 | tf_op jit(solution)/shard_map/ppermute | solution.py:52
  80.4 7.0 %collective-permute-start.24 = (bf16[4,96,256]{2,1,0:T(8,128)(2,1)S(1)}, bf16[4,96,256]{2,1,0:T(8,128)(2,1)S(1)}, u32[]{:S(2)}, u32[]{:S(2)}) collective-permute-start(bf16[4,96,256]{2,1,0:T(8,128)(2,1)S(1)} %get-tuple-element.92), channel_id=1, source_target_pairs={{0,8},{1,25},{8,0},{9,17},{16,24},{17,9},{24,16},{25,1},{2,10},{3,... | collective-permute-start | bytes 589832 | tf_op jit(solution)/shard_map/ppermute | solution.py:52
  80.5 11.6 %collective-permute-start.25 = (bf16[4,96,256]{2,1,0:T(8,128)(2,1)S(1)}, bf16[4,96,256]{2,1,0:T(8,128)(2,1)S(1)}, u32[]{:S(2)}, u32[]{:S(2)}) collective-permute-start(bf16[4,96,256]{2,1,0:T(8,128)(2,1)S(1)} %get-tuple-element.93), channel_id=1, source_target_pairs={{0,16},{1,17},{8,24},{9,25},{16,0},{17,1},{24,8},{25,9},{2,18},{3,... | collective-permute-start | bytes 589832 | tf_op jit(solution)/shard_map/ppermute | solution.py:52
  82.9 9.9 %collective-permute-start.26 = (bf16[4,96,256]{2,1,0:T(8,128)(2,1)S(1)}, bf16[4,96,256]{2,1,0:T(8,128)(2,1)S(1)}, u32[]{:S(2)}, u32[]{:S(2)}) collective-permute-start(bf16[4,96,256]{2,1,0:T(8,128)(2,1)S(1)} %get-tuple-element.94), channel_id=1, source_target_pairs={{0,24},{1,9},{8,16},{9,1},{16,8},{17,25},{24,0},{25,17},{2,26},{3,... | collective-permute-start | bytes 589832 | tf_op jit(solution)/shard_map/ppermute | solution.py:52
  92.8 6.6 %collective-permute-start.27 = (bf16[96,256]{1,0:T(8,128)(2,1)S(1)}, bf16[96,256]{1,0:T(8,128)(2,1)S(1)}, u32[]{:S(2)}, u32[]{:S(2)}) collective-permute-start(bf16[96,256]{1,0:T(8,128)(2,1)S(1)} %get-tuple-element.96), channel_id=1, source_target_pairs={{0,2},{1,7},{2,0},{3,5},{4,6},{5,3},{6,4},{7,1},{8,10},{9,15},{10,... | collective-permute-start | bytes 147464 | tf_op jit(solution)/shard_map/ppermute | solution.py:52
  93.9 8.2 %collective-permute-start.28 = (bf16[96,256]{1,0:T(8,128)(2,1)S(1)}, bf16[96,256]{1,0:T(8,128)(2,1)S(1)}, u32[]{:S(2)}, u32[]{:S(2)}) collective-permute-start(bf16[96,256]{1,0:T(8,128)(2,1)S(1)} %get-tuple-element.97), channel_id=1, source_target_pairs={{0,4},{1,5},{2,6},{3,7},{4,0},{5,1},{6,2},{7,3},{8,12},{9,13},{10,... | collective-permute-start | bytes 147464 | tf_op jit(solution)/shard_map/ppermute | solution.py:52
  97.0 6.2 %collective-permute-start.29 = (bf16[96,256]{1,0:T(8,128)(2,1)S(1)}, bf16[96,256]{1,0:T(8,128)(2,1)S(1)}, u32[]{:S(2)}, u32[]{:S(2)}) collective-permute-start(bf16[96,256]{1,0:T(8,128)(2,1)S(1)} %get-tuple-element.98), channel_id=1, source_target_pairs={{0,6},{1,3},{2,4},{3,1},{4,2},{5,7},{6,0},{7,5},{8,14},{9,11},{10,... | collective-permute-start | bytes 147464 | tf_op jit(solution)/shard_map/ppermute | solution.py:52
  103.5 6.6 %collective-permute-start.32 = (bf16[96,256]{1,0:T(8,128)(2,1)S(1)}, bf16[96,256]{1,0:T(8,128)(2,1)S(1)}, u32[]{:S(2)}, u32[]{:S(2)}) collective-permute-start(bf16[96,256]{1,0:T(8,128)(2,1)S(1)} %get-tuple-element.99), channel_id=1, source_target_pairs={{0,6},{1,3},{2,4},{3,1},{4,2},{5,7},{6,0},{7,5},{8,14},{9,11},{10,... | collective-permute-start | bytes 147464 | tf_op jit(solution)/shard_map/ppermute | solution.py:52
  106.3 8.0 %collective-permute-start.31 = (bf16[96,256]{1,0:T(8,128)(2,1)S(1)}, bf16[96,256]{1,0:T(8,128)(2,1)S(1)}, u32[]{:S(2)}, u32[]{:S(2)}) collective-permute-start(bf16[96,256]{1,0:T(8,128)(2,1)S(1)} %get-tuple-element.99), channel_id=1, source_target_pairs={{0,4},{1,5},{2,6},{3,7},{4,0},{5,1},{6,2},{7,3},{8,12},{9,13},{10,... | collective-permute-start | bytes 147464 | tf_op jit(solution)/shard_map/ppermute | solution.py:52
  109.1 5.5 %collective-permute-start.30 = (bf16[96,256]{1,0:T(8,128)(2,1)S(1)}, bf16[96,256]{1,0:T(8,128)(2,1)S(1)}, u32[]{:S(2)}, u32[]{:S(2)}) collective-permute-start(bf16[96,256]{1,0:T(8,128)(2,1)S(1)} %get-tuple-element.99), channel_id=1, source_target_pairs={{0,2},{1,7},{2,0},{3,5},{4,6},{5,3},{6,4},{7,1},{8,10},{9,15},{10,... | collective-permute-start | bytes 147464 | tf_op jit(solution)/shard_map/ppermute | solution.py:52
  114.7 12.1 %collective-permute-start.36 = (bf16[4,96,256]{2,1,0:T(8,128)(2,1)S(1)}, bf16[4,96,256]{2,1,0:T(8,128)(2,1)S(1)}, u32[]{:S(2)}, u32[]{:S(2)}) collective-permute-start(bf16[4,96,256]{2,1,0:T(8,128)(2,1)S(1)} %pad_maximum_fusion.2.refs_0_), channel_id=1, source_target_pairs={{0,24},{1,9},{8,16},{9,1},{16,8},{17,25},{24,0},{25,17},{2,26},{3,... | collective-permute-start | bytes 589832 | tf_op jit(solution)/shard_map/ppermute | solution.py:52
  116.8 10.0 %collective-permute-start.35 = (bf16[4,96,256]{2,1,0:T(8,128)(2,1)S(1)}, bf16[4,96,256]{2,1,0:T(8,128)(2,1)S(1)}, u32[]{:S(2)}, u32[]{:S(2)}) collective-permute-start(bf16[4,96,256]{2,1,0:T(8,128)(2,1)S(1)} %pad_maximum_fusion.2.refs_0_), channel_id=1, source_target_pairs={{0,16},{1,17},{8,24},{9,25},{16,0},{17,1},{24,8},{25,9},{2,18},{3,... | collective-permute-start | bytes 589832 | tf_op jit(solution)/shard_map/ppermute | solution.py:52
  116.8 10.0 %collective-permute-start.34 = (bf16[4,96,256]{2,1,0:T(8,128)(2,1)S(1)}, bf16[4,96,256]{2,1,0:T(8,128)(2,1)S(1)}, u32[]{:S(2)}, u32[]{:S(2)}) collective-permute-start(bf16[4,96,256]{2,1,0:T(8,128)(2,1)S(1)} %pad_maximum_fusion.2.refs_0_), channel_id=1, source_target_pairs={{0,8},{1,25},{8,0},{9,17},{16,24},{17,9},{24,16},{25,1},{2,10},{3,... | collective-permute-start | bytes 589832 | tf_op jit(solution)/shard_map/ppermute | solution.py:52
  118.8 1.3 collective-permute-start.1
  118.8 3.2 %collective-permute-start.23 = (bf16[256,256]{1,0:T(8,128)(2,1)S(1)}, bf16[256,256]{1,0:T(8,128)(2,1)S(1)}, u32[]{:S(2)}, u32[]{:S(2)}) collective-permute-start(bf16[256,256]{1,0:T(8,128)(2,1)S(1)} %get-tuple-element.89), channel_id=1, source_target_pairs={{0,1},{1,0},{2,3},{3,2},{4,5},{5,4},{6,7},{7,6},{8,9},{9,8},{10,11... | collective-permute-start | bytes 393224 | tf_op jit(solution)/shard_map/ppermute | solution.py:281
  120.2 1.2 collective-permute-start.33
  127.7 1.5 %collective-permute-start.38 = (f32[8,256]{1,0:T(8,128)S(1)}, f32[8,256]{1,0:T(8,128)S(1)}, u32[]{:S(2)}, u32[]{:S(2)}) collective-permute-start(f32[8,256]{1,0:T(8,128)S(1)} %fusion.3), channel_id=1, source_target_pairs={{0,1},{1,0},{2,3},{3,2},{4,5},{5,4},{6,7},{7,6},{8,9},{9,8},{10,11... | collective-permute-start | bytes 24584 | tf_op jit(solution)/shard_map/ppermute | solution.py:281
  129.2 4.9 %collective-permute-start.41 = (f32[8,256]{1,0:T(8,128)S(1)}, f32[8,256]{1,0:T(8,128)S(1)}, u32[]{:S(2)}, u32[]{:S(2)}) collective-permute-start(f32[8,256]{1,0:T(8,128)S(1)} %fusion.2), channel_id=1, source_target_pairs={{0,96},{1,33},{32,64},{33,1},{64,32},{65,97},{96,0},{97,65},{2,98}... | collective-permute-start | bytes 24584 | tf_op jit(solution)/shard_map/ppermute | solution.py:52
  132.2 5.2 %collective-permute-start.40 = (f32[8,256]{1,0:T(8,128)S(1)}, f32[8,256]{1,0:T(8,128)S(1)}, u32[]{:S(2)}, u32[]{:S(2)}) collective-permute-start(f32[8,256]{1,0:T(8,128)S(1)} %fusion.2), channel_id=1, source_target_pairs={{0,64},{1,65},{32,96},{33,97},{64,0},{65,1},{96,32},{97,33},{2,66}... | collective-permute-start | bytes 24584 | tf_op jit(solution)/shard_map/ppermute | solution.py:52
  132.8 4.5 %collective-permute-start.39 = (f32[8,256]{1,0:T(8,128)S(1)}, f32[8,256]{1,0:T(8,128)S(1)}, u32[]{:S(2)}, u32[]{:S(2)}) collective-permute-start(f32[8,256]{1,0:T(8,128)S(1)} %fusion.2), channel_id=1, source_target_pairs={{0,32},{1,97},{32,0},{33,65},{64,96},{65,33},{96,64},{97,1},{2,34}... | collective-permute-start | bytes 24584 | tf_op jit(solution)/shard_map/ppermute | solution.py:52
  133.4 7.7 %collective-permute-start.22 = (bf16[256,256]{1,0:T(8,128)(2,1)S(1)}, bf16[256,256]{1,0:T(8,128)(2,1)S(1)}, u32[]{:S(2)}, u32[]{:S(2)}) collective-permute-start(bf16[256,256]{1,0:T(8,128)(2,1)S(1)} %get-tuple-element.87), channel_id=1, source_target_pairs={{0,1},{1,0},{2,3},{3,2},{4,5},{5,4},{6,7},{7,6},{8,9},{9,8},{10,11... | collective-permute-start | bytes 393224 | tf_op jit(solution)/shard_map/ppermute | solution.py:281
  133.4 7.7 %collective-permute-start.37 = (bf16[256,256]{1,0:T(8,128)(2,1)S(1)}, bf16[256,256]{1,0:T(8,128)(2,1)S(1)}, u32[]{:S(2)}, u32[]{:S(2)}) collective-permute-start(bf16[256,256]{1,0:T(8,128)(2,1)S(1)} %get-tuple-element.107), channel_id=1, source_target_pairs={{0,1},{1,0},{2,3},{3,2},{4,5},{5,4},{6,7},{7,6},{8,9},{9,8},{10,11... | collective-permute-start | bytes 393224 | tf_op jit(solution)/shard_map/ppermute | solution.py:281
  137.4 3.7 %collective-permute-start.42 = (f32[8,256]{1,0:T(8,128)S(1)}, f32[8,256]{1,0:T(8,128)S(1)}, u32[]{:S(2)}, u32[]{:S(2)}) collective-permute-start(f32[8,256]{1,0:T(8,128)S(1)} %add_add_fusion), channel_id=1, source_target_pairs={{0,128},{128,0},{1,129},{129,1},{2,130},{130,2},{3,131},{131,3},{4... | collective-permute-start | bytes 24584 | tf_op jit(solution)/shard_map/ppermute | solution.py:277
where the time goes:
time: 143 us
  waiting for transfers between devices  69.1 us (48%)
  starting transfers between devices  63 us (44%)
  Pallas kernels  9.59 us (7%)
    ppermute x33, waiting for transfers between devices, shift(): return lax.ppermute(array, (axis, 'core'), pairs)  62.1 us
    ppermute x33, starting transfers between devices, shift(): return lax.ppermute(array, (axis, 'core'), pairs)  61.2 us
    pallas_call x13, Pallas kernels, call(): pl.pallas_call(kernel, in_specs=[SMEM] * len(scalars) + [VMEM] * (len(hel...  9.59 us
    ppermute x1, waiting for transfers between devices, head_sum(): return sq + lax.ppermute(sq, 'hz', SWAP)  3.64 us
    ppermute x9, waiting for transfers between devices, swap(): return lax.ppermute(array, 'core', SWAP)  3.39 us
  transfers between devices with their start and end apart: 43, of which 25 were waited for; matrix products, arithmetic and copies ran while one was open for 0% of the time, Pallas kernels for 2%

commit v1 on v0

--- a/solution.py
+++ b/solution.py
@@ -109,6 +109,7 @@
 
 def tokens_kernel(counts, queries, keys, values, rates, gain_in, *outs):
     outs[8][...] = gain_in[...]
+    masks = outs[9]
     ke_own, q_own, ke_out, q_out = outs[0:2], outs[2:4], outs[4:6], outs[6:8]
     tx, tz, core = position()
     tok = (tx * NZ + tz) * 2 + core
@@ -117,6 +118,7 @@
     for head, sends in ((core, False), (1 - core, True)):
         for g in range(2):
             valid = (lane < counts[g, tok]).astype(f32)
+            masks[g : g + 1, :] = valid
             both = rates[g].astype(f32)
             row = jnp.where(head == 0, both[0:1], both[1:2]) * grad_scale * valid
             col = jnp.broadcast_to(row, (128, BLK)).T
@@ -248,13 +250,11 @@
     )
 
 
-def finish_kernel(counts, o0, r0, o1, r1, sq, gain, out):
-    tx, tz, core = position()
-    tok = (tx * NZ + tz) * 2 + core
+def finish_kernel(o0, r0, o1, r1, sq, gain, masks, out):
+    core = position()[2]
     for g, (own, other) in enumerate(((o0, r0), (o1, r1))):
-        valid = lax.broadcasted_iota(jnp.int32, (1, BLK), 1) < counts[g, tok]
         row = lax.rsqrt(sq[4 * g : 4 * g + 1, :] * (1.0 / (HEADS * DH)) + EPS)
-        scale = jnp.broadcast_to(jnp.where(valid, row, 0.0), (128, BLK)).T
+        scale = jnp.broadcast_to(row * masks[g : g + 1, :], (128, BLK)).T
         scale = jnp.concatenate([scale, scale], axis=1)
         for head, o in ((core, own), (1 - core, other)):
             out[g, head] = (o[...].astype(f32) * gain[pl.ds(head, 1), :] * scale).astype(bf16)
@@ -296,7 +296,7 @@
     got = call(
         tokens_kernel,
         (),
-        [pair, pair, single, single] * 2 + [on_chip((2, DH), f32)],
+        [pair, pair, single, single] * 2 + [on_chip((2, DH), f32), on_chip((2, BLK), f32)],
         scalars=(counts,),
         hbm=(*tokens, out_gain),
         limit=16,
@@ -330,9 +330,8 @@
     r1 = swap(o1_send)
     (mixed,) = call(
         finish_kernel,
-        (o0, r0, o1, r1, total, got[8]),
+        (o0, r0, o1, r1, total, got[8], got[9]),
         [jax.ShapeDtypeStruct((2, 2, BLK, DH), bf16)],
-        scalars=(counts,),
     )
     return (mixed, *finals)
 

time: 143 us -> 142 us (level)
  no operation moved by 1% of the time
where the time goes in v1:
time: 142 us
  waiting for transfers between devices  69.1 us (49%)
  starting transfers between devices  63 us (44%)
  Pallas kernels  9.04 us (6%)
    ppermute x33, waiting for transfers between devices, shift(): return lax.ppermute(array, (axis, 'core'), pairs)  62.1 us
    ppermute x33, starting transfers between devices, shift(): return lax.ppermute(array, (axis, 'core'), pairs)  61.2 us
    pallas_call x13, Pallas kernels, call(): pl.pallas_call(kernel, in_specs=[SMEM] * len(scalars) + [VMEM] * (len(hel...  9.04 us
    ppermute x1, waiting for transfers between devices, head_sum(): return sq + lax.ppermute(sq, 'hz', SWAP)  3.64 us
    ppermute x9, waiting for transfers between devices, swap(): return lax.ppermute(array, 'core', SWAP)  3.39 us
  transfers between devices with their start and end apart: 43, of which 25 were waited for; matrix products, arithmetic and copies ran while one was open for 0% of the time, Pallas kernels for 2%

profile of v1, /device:TPU:32, one launch (start us, length us, event | category | flops | bytes accessed | tf_op | source)
XLA Modules:
  0.0 142.1 jit_solution(12561356503054072967)
XLA Ops:
  0.6 0.8 shard_map.120
  1.5 1.2 collective-permute-done.recv
  2.8 5.5 %collective-permute-start.6 = (bf16[96,256]{1,0:T(8,128)(2,1)S(1)}, bf16[96,256]{1,0:T(8,128)(2,1)S(1)}, u32[]{:S(2)}, u32[]{:S(2)}) collective-permute-start(bf16[96,256]{1,0:T(8,128)(2,1)S(1)} %get-tuple-element.74), channel_id=1, source_target_pairs={{0,6},{1,3},{2,4},{3,1},{4,2},{5,7},{6,0},{7,5},{8,14},{9,11},{10,... | collective-permute-start | bytes 147464 | tf_op jit(solution)/shard_map/ppermute | solution.py:52
  8.3 1.4 %collective-permute-start.5 = (bf16[96,256]{1,0:T(8,128)(2,1)S(1)}, bf16[96,256]{1,0:T(8,128)(2,1)S(1)}, u32[]{:S(2)}, u32[]{:S(2)}) collective-permute-start(bf16[96,256]{1,0:T(8,128)(2,1)S(1)} %get-tuple-element.74), channel_id=1, source_target_pairs={{0,4},{1,5},{2,6},{3,7},{4,0},{5,1},{6,2},{7,3},{8,12},{9,13},{10,... | collective-permute-start | bytes 147464 | tf_op jit(solution)/shard_map/ppermute | solution.py:52
  9.7 1.0 collective-permute-start.4
  10.7 1.6 %shard_map.122 = (bf16[2,256,256]{2,1,0:T(8,128)(2,1)S(1)}, bf16[2,256,256]{2,1,0:T(8,128)(2,1)S(1)}, bf16[256,256]{1,0:T(8,128)(2,1)S(1)}, bf16[256,256]{1,0:T(...) custom-call(s32[2,32]{1,0:T(2,128)S(1)} %copy-done, ...), custom_call_target="tpu_custom_call" | custom-call | tf_op jit(solution)/shard_map/pallas_call | solution.py:34
  12.5 4.3 %collective-permute-done.5 = bf16[96,256]{1,0:T(8,128)(2,1)S(1)} collective-permute-done((bf16[96,256]{1,0:T(8,128)(2,1)S(1)}, bf16[96,256]{1,0:T(8,128)(2,1)S(1)}, u32[]{:S(2)}, u32[]{:S(2)}) %collective-permute-start.5) | collective-permute-done | bytes 49184 | tf_op jit(solution)/shard_map/ppermute | solution.py:52
  16.8 2.8 %collective-permute-start.9 = (bf16[4,96,256]{2,1,0:T(8,128)(2,1)S(1)}, bf16[4,96,256]{2,1,0:T(8,128)(2,1)S(1)}, u32[]{:S(2)}, u32[]{:S(2)}) collective-permute-start(bf16[4,96,256]{2,1,0:T(8,128)(2,1)S(1)} %pad_maximum_fusion.s0), channel_id=1, source_target_pairs={{0,24},{1,9},{8,16},{9,1},{16,8},{17,25},{24,0},{25,17},{2,26},{3,... | collective-permute-start | bytes 589832 | tf_op jit(solution)/shard_map/ppermute | solution.py:52
  19.7 0.8 collective-permute-start.8
  20.5 0.5 collective-permute-start.7
  21.0 7.9 %collective-permute-done.9.s3 = bf16[4,96,256]{2,1,0:T(8,128)(2,1)S(1)} collective-permute-done((bf16[4,96,256]{2,1,0:T(8,128)(2,1)S(1)}, bf16[4,96,256]{2,1,0:T(8,128)(2,1)S(1)}, u32[]{:S(2)}, u32[]{:S(2)}) %collective-permute-start.9) | collective-permute-done | bytes 196640 | tf_op jit(solution)/shard_map/ppermute | solution.py:52
  28.9 1.3 shard_map.123
  30.2 0.9 collective-permute-start.10
  31.1 4.4 %collective-permute-start.11 = (bf16[4,96,256]{2,1,0:T(8,128)(2,1)S(1)}, bf16[4,96,256]{2,1,0:T(8,128)(2,1)S(1)}, u32[]{:S(2)}, u32[]{:S(2)}) collective-permute-start(bf16[4,96,256]{2,1,0:T(8,128)(2,1)S(1)} %get-tuple-element.77), channel_id=1, source_target_pairs={{0,16},{1,17},{8,24},{9,25},{16,0},{17,1},{24,8},{25,9},{2,18},{3,... | collective-permute-start | bytes 589832 | tf_op jit(solution)/shard_map/ppermute | solution.py:52
  35.5 0.7 collective-permute-done.10.r1
  36.2 8.3 %collective-permute-done.11.r2 = bf16[4,96,256]{2,1,0:T(8,128)(2,1)S(1)} collective-permute-done((bf16[4,96,256]{2,1,0:T(8,128)(2,1)S(1)}, bf16[4,96,256]{2,1,0:T(8,128)(2,1)S(1)}, u32[]{:S(2)}, u32[]{:S(2)}) %collective-permute-start.11) | collective-permute-done | bytes 196640 | tf_op jit(solution)/shard_map/ppermute | solution.py:52
  44.5 0.9 collective-permute-done.12.r3
  45.5 0.9 collective-permute-start.13
  46.4 2.9 %collective-permute-start.14 = (bf16[96,256]{1,0:T(8,128)(2,1)S(1)}, bf16[96,256]{1,0:T(8,128)(2,1)S(1)}, u32[]{:S(2)}, u32[]{:S(2)}) collective-permute-start(bf16[96,256]{1,0:T(8,128)(2,1)S(1)} %get-tuple-element.81), channel_id=1, source_target_pairs={{0,4},{1,5},{2,6},{3,7},{4,0},{5,1},{6,2},{7,3},{8,12},{9,13},{10,... | collective-permute-start | bytes 147464 | tf_op jit(solution)/shard_map/ppermute | solution.py:52
  49.3 2.8 %collective-permute-start.15 = (bf16[96,256]{1,0:T(8,128)(2,1)S(1)}, bf16[96,256]{1,0:T(8,128)(2,1)S(1)}, u32[]{:S(2)}, u32[]{:S(2)}) collective-permute-start(bf16[96,256]{1,0:T(8,128)(2,1)S(1)} %get-tuple-element.82), channel_id=1, source_target_pairs={{0,6},{1,3},{2,4},{3,1},{4,2},{5,7},{6,0},{7,5},{8,14},{9,11},{10,... | collective-permute-start | bytes 147464 | tf_op jit(solution)/shard_map/ppermute | solution.py:52
  52.1 2.5 %collective-permute-done.14.t2 = bf16[96,256]{1,0:T(8,128)(2,1)S(1)} collective-permute-done((bf16[96,256]{1,0:T(8,128)(2,1)S(1)}, bf16[96,256]{1,0:T(8,128)(2,1)S(1)}, u32[]{:S(2)}, u32[]{:S(2)}) %collective-permute-start.14) | collective-permute-done | bytes 49184 | tf_op jit(solution)/shard_map/ppermute | solution.py:52
  54.6 1.9 %collective-permute-done.15.t3 = bf16[96,256]{1,0:T(8,128)(2,1)S(1)} collective-permute-done((bf16[96,256]{1,0:T(8,128)(2,1)S(1)}, bf16[96,256]{1,0:T(8,128)(2,1)S(1)}, u32[]{:S(2)}, u32[]{:S(2)}) %collective-permute-start.15) | collective-permute-done | bytes 49184 | tf_op jit(solution)/shard_map/ppermute | solution.py:52
  56.8 1.8 %collective-permute-start.18 = (bf16[96,256]{1,0:T(8,128)(2,1)S(1)}, bf16[96,256]{1,0:T(8,128)(2,1)S(1)}, u32[]{:S(2)}, u32[]{:S(2)}) collective-permute-start(bf16[96,256]{1,0:T(8,128)(2,1)S(1)} %get-tuple-element.83), channel_id=1, source_target_pairs={{0,6},{1,3},{2,4},{3,1},{4,2},{5,7},{6,0},{7,5},{8,14},{9,11},{10,... | collective-permute-start | bytes 147464 | tf_op jit(solution)/shard_map/ppermute | solution.py:52
  58.6 2.9 %collective-permute-start.17 = (bf16[96,256]{1,0:T(8,128)(2,1)S(1)}, bf16[96,256]{1,0:T(8,128)(2,1)S(1)}, u32[]{:S(2)}, u32[]{:S(2)}) collective-permute-start(bf16[96,256]{1,0:T(8,128)(2,1)S(1)} %get-tuple-element.83), channel_id=1, source_target_pairs={{0,4},{1,5},{2,6},{3,7},{4,0},{5,1},{6,2},{7,3},{8,12},{9,13},{10,... | collective-permute-start | bytes 147464 | tf_op jit(solution)/shard_map/ppermute | solution.py:52
  61.4 1.9 %collective-permute-start.16 = (bf16[96,256]{1,0:T(8,128)(2,1)S(1)}, bf16[96,256]{1,0:T(8,128)(2,1)S(1)}, u32[]{:S(2)}, u32[]{:S(2)}) collective-permute-start(bf16[96,256]{1,0:T(8,128)(2,1)S(1)} %get-tuple-element.83), channel_id=1, source_target_pairs={{0,2},{1,7},{2,0},{3,5},{4,6},{5,3},{6,4},{7,1},{8,10},{9,15},{10,... | collective-permute-start | bytes 147464 | tf_op jit(solution)/shard_map/ppermute | solution.py:52
  63.4 3.7 %collective-permute-done.17 = bf16[96,256]{1,0:T(8,128)(2,1)S(1)} collective-permute-done((bf16[96,256]{1,0:T(8,128)(2,1)S(1)}, bf16[96,256]{1,0:T(8,128)(2,1)S(1)}, u32[]{:S(2)}, u32[]{:S(2)}) %collective-permute-start.17) | collective-permute-done | bytes 49184 | tf_op jit(solution)/shard_map/ppermute | solution.py:52
  67.1 1.8 %collective-permute-start.21 = (bf16[4,96,256]{2,1,0:T(8,128)(2,1)S(1)}, bf16[4,96,256]{2,1,0:T(8,128)(2,1)S(1)}, u32[]{:S(2)}, u32[]{:S(2)}) collective-permute-start(bf16[4,96,256]{2,1,0:T(8,128)(2,1)S(1)} %pad_maximum_fusion.1.s0), channel_id=1, source_target_pairs={{0,24},{1,9},{8,16},{9,1},{16,8},{17,25},{24,0},{25,17},{2,26},{3,... | collective-permute-start | bytes 589832 | tf_op jit(solution)/shard_map/ppermute | solution.py:52
  69.0 2.5 %collective-permute-start.19 = (bf16[4,96,256]{2,1,0:T(8,128)(2,1)S(1)}, bf16[4,96,256]{2,1,0:T(8,128)(2,1)S(1)}, u32[]{:S(2)}, u32[]{:S(2)}) collective-permute-start(bf16[4,96,256]{2,1,0:T(8,128)(2,1)S(1)} %pad_maximum_fusion.1.s0), channel_id=1, source_target_pairs={{0,8},{1,25},{8,0},{9,17},{16,24},{17,9},{24,16},{25,1},{2,10},{3,... | collective-permute-start | bytes 589832 | tf_op jit(solution)/shard_map/ppermute | solution.py:52
  71.5 7.5 %collective-permute-done.21.s3 = bf16[4,96,256]{2,1,0:T(8,128)(2,1)S(1)} collective-permute-done((bf16[4,96,256]{2,1,0:T(8,128)(2,1)S(1)}, bf16[4,96,256]{2,1,0:T(8,128)(2,1)S(1)}, u32[]{:S(2)}, u32[]{:S(2)}) %collective-permute-start.21) | collective-permute-done | bytes 196640 | tf_op jit(solution)/shard_map/ppermute | solution.py:52
  79.1 1.3 shard_map.126
  80.5 2.4 %collective-permute-start.25 = (bf16[4,96,256]{2,1,0:T(8,128)(2,1)S(1)}, bf16[4,96,256]{2,1,0:T(8,128)(2,1)S(1)}, u32[]{:S(2)}, u32[]{:S(2)}) collective-permute-start(bf16[4,96,256]{2,1,0:T(8,128)(2,1)S(1)} %get-tuple-element.94), channel_id=1, source_target_pairs={{0,16},{1,17},{8,24},{9,25},{16,0},{17,1},{24,8},{25,9},{2,18},{3,... | collective-permute-start | bytes 589832 | tf_op jit(solution)/shard_map/ppermute | solution.py:52
  82.9 2.3 %collective-permute-start.26 = (bf16[4,96,256]{2,1,0:T(8,128)(2,1)S(1)}, bf16[4,96,256]{2,1,0:T(8,128)(2,1)S(1)}, u32[]{:S(2)}, u32[]{:S(2)}) collective-permute-start(bf16[4,96,256]{2,1,0:T(8,128)(2,1)S(1)} %get-tuple-element.95), channel_id=1, source_target_pairs={{0,24},{1,9},{8,16},{9,1},{16,8},{17,25},{24,0},{25,17},{2,26},{3,... | collective-permute-start | bytes 589832 | tf_op jit(solution)/shard_map/ppermute | solution.py:52
  85.2 2.2 %collective-permute-done.24.r1 = bf16[4,96,256]{2,1,0:T(8,128)(2,1)S(1)} collective-permute-done((bf16[4,96,256]{2,1,0:T(8,128)(2,1)S(1)}, bf16[4,96,256]{2,1,0:T(8,128)(2,1)S(1)}, u32[]{:S(2)}, u32[]{:S(2)}) %collective-permute-start.24) | collective-permute-done | bytes 196640 | tf_op jit(solution)/shard_map/ppermute | solution.py:52
  87.4 4.6 %collective-permute-done.25.r2 = bf16[4,96,256]{2,1,0:T(8,128)(2,1)S(1)} collective-permute-done((bf16[4,96,256]{2,1,0:T(8,128)(2,1)S(1)}, bf16[4,96,256]{2,1,0:T(8,128)(2,1)S(1)}, u32[]{:S(2)}, u32[]{:S(2)}) %collective-permute-start.25) | collective-permute-done | bytes 196640 | tf_op jit(solution)/shard_map/ppermute | solution.py:52
  92.0 0.7 collective-permute-done.26.r3
  92.8 1.1 collective-permute-start.27
  93.9 3.1 %collective-permute-start.28 = (bf16[96,256]{1,0:T(8,128)(2,1)S(1)}, bf16[96,256]{1,0:T(8,128)(2,1)S(1)}, u32[]{:S(2)}, u32[]{:S(2)}) collective-permute-start(bf16[96,256]{1,0:T(8,128)(2,1)S(1)} %get-tuple-element.98), channel_id=1, source_target_pairs={{0,4},{1,5},{2,6},{3,7},{4,0},{5,1},{6,2},{7,3},{8,12},{9,13},{10,... | collective-permute-start | bytes 147464 | tf_op jit(solution)/shard_map/ppermute | solution.py:52
  97.0 2.4 %collective-permute-start.29 = (bf16[96,256]{1,0:T(8,128)(2,1)S(1)}, bf16[96,256]{1,0:T(8,128)(2,1)S(1)}, u32[]{:S(2)}, u32[]{:S(2)}) collective-permute-start(bf16[96,256]{1,0:T(8,128)(2,1)S(1)} %get-tuple-element.99), channel_id=1, source_target_pairs={{0,6},{1,3},{2,4},{3,1},{4,2},{5,7},{6,0},{7,5},{8,14},{9,11},{10,... | collective-permute-start | bytes 147464 | tf_op jit(solution)/shard_map/ppermute | solution.py:52
  99.4 2.7 %collective-permute-done.28.t2 = bf16[96,256]{1,0:T(8,128)(2,1)S(1)} collective-permute-done((bf16[96,256]{1,0:T(8,128)(2,1)S(1)}, bf16[96,256]{1,0:T(8,128)(2,1)S(1)}, u32[]{:S(2)}, u32[]{:S(2)}) %collective-permute-start.28) | collective-permute-done | bytes 49184 | tf_op jit(solution)/shard_map/ppermute | solution.py:52
  102.1 1.1 collective-permute-done.29.t3
  103.3 0.2 shard_map.129
  103.5 2.8 %collective-permute-start.32 = (bf16[96,256]{1,0:T(8,128)(2,1)S(1)}, bf16[96,256]{1,0:T(8,128)(2,1)S(1)}, u32[]{:S(2)}, u32[]{:S(2)}) collective-permute-start(bf16[96,256]{1,0:T(8,128)(2,1)S(1)} %get-tuple-element.100), channel_id=1, source_target_pairs={{0,6},{1,3},{2,4},{3,1},{4,2},{5,7},{6,0},{7,5},{8,14},{9,11},{10,... | collective-permute-start | bytes 147464 | tf_op jit(solution)/shard_map/ppermute | solution.py:52
  106.3 2.8 %collective-permute-start.31 = (bf16[96,256]{1,0:T(8,128)(2,1)S(1)}, bf16[96,256]{1,0:T(8,128)(2,1)S(1)}, u32[]{:S(2)}, u32[]{:S(2)}) collective-permute-start(bf16[96,256]{1,0:T(8,128)(2,1)S(1)} %get-tuple-element.100), channel_id=1, source_target_pairs={{0,4},{1,5},{2,6},{3,7},{4,0},{5,1},{6,2},{7,3},{8,12},{9,13},{10,... | collective-permute-start | bytes 147464 | tf_op jit(solution)/shard_map/ppermute | solution.py:52
  109.1 1.0 collective-permute-start.30
  110.1 4.2 %collective-permute-done.31 = bf16[96,256]{1,0:T(8,128)(2,1)S(1)} collective-permute-done((bf16[96,256]{1,0:T(8,128)(2,1)S(1)}, bf16[96,256]{1,0:T(8,128)(2,1)S(1)}, u32[]{:S(2)}, u32[]{:S(2)}) %collective-permute-start.31) | collective-permute-done | bytes 49184 | tf_op jit(solution)/shard_map/ppermute | solution.py:52
  114.3 0.3 collective-permute-done.30
  114.7 2.1 %collective-permute-start.36 = (bf16[4,96,256]{2,1,0:T(8,128)(2,1)S(1)}, bf16[4,96,256]{2,1,0:T(8,128)(2,1)S(1)}, u32[]{:S(2)}, u32[]{:S(2)}) collective-permute-start(bf16[4,96,256]{2,1,0:T(8,128)(2,1)S(1)} %pad_maximum_fusion.2.refs_0_), channel_id=1, source_target_pairs={{0,24},{1,9},{8,16},{9,1},{16,8},{17,25},{24,0},{25,17},{2,26},{3,... | collective-permute-start | bytes 589832 | tf_op jit(solution)/shard_map/ppermute | solution.py:52
  116.8 2.1 %collective-permute-start.34 = (bf16[4,96,256]{2,1,0:T(8,128)(2,1)S(1)}, bf16[4,96,256]{2,1,0:T(8,128)(2,1)S(1)}, u32[]{:S(2)}, u32[]{:S(2)}) collective-permute-start(bf16[4,96,256]{2,1,0:T(8,128)(2,1)S(1)} %pad_maximum_fusion.2.refs_0_), channel_id=1, source_target_pairs={{0,8},{1,25},{8,0},{9,17},{16,24},{17,9},{24,16},{25,1},{2,10},{3,... | collective-permute-start | bytes 589832 | tf_op jit(solution)/shard_map/ppermute | solution.py:52
  118.8 0.5 collective-permute-start.23
  119.4 0.8 collective-permute-done.1.q_other
  120.3 0.9 shard_map.127
  121.4 0.6 shard_map.130
  122.1 4.7 %collective-permute-done.36.refs_3_ = bf16[4,96,256]{2,1,0:T(8,128)(2,1)S(1)} collective-permute-done((bf16[4,96,256]{2,1,0:T(8,128)(2,1)S(1)}, bf16[4,96,256]{2,1,0:T(8,128)(2,1)S(1)}, u32[]{:S(2)}, u32[]{:S(2)}) %collective-permute-start.36) | collective-permute-done | bytes 196640 | tf_op jit(solution)/shard_map/ppermute | solution.py:52
  126.8 0.9 shard_map.131
  127.7 0.3 collective-permute-start.38
  128.1 1.1 collective-permute-done.38
  129.2 3.0 %collective-permute-start.41 = (f32[8,256]{1,0:T(8,128)S(1)}, f32[8,256]{1,0:T(8,128)S(1)}, u32[]{:S(2)}, u32[]{:S(2)}) collective-permute-start(f32[8,256]{1,0:T(8,128)S(1)} %fusion.2), channel_id=1, source_target_pairs={{0,96},{1,33},{32,64},{33,1},{64,32},{65,97},{96,0},{97,65},{2,98}... | collective-permute-start | bytes 24584 | tf_op jit(solution)/shard_map/ppermute | solution.py:52
  132.2 0.6 collective-permute-start.40
  132.8 0.6 collective-permute-start.39
  133.4 0.5 collective-permute-start.37
  133.9 0.3 collective-permute-done.41
  134.2 3.2 %collective-permute-done.40 = f32[8,256]{1,0:T(8,128)S(1)} collective-permute-done((f32[8,256]{1,0:T(8,128)S(1)}, f32[8,256]{1,0:T(8,128)S(1)}, u32[]{:S(2)}, u32[]{:S(2)}) %collective-permute-start.40) | collective-permute-done | bytes 8224 | tf_op jit(solution)/shard_map/ppermute | solution.py:52
  137.5 3.6 %collective-permute-done.42 = f32[8,256]{1,0:T(8,128)S(1)} collective-permute-done((f32[8,256]{1,0:T(8,128)S(1)}, f32[8,256]{1,0:T(8,128)S(1)}, u32[]{:S(2)}, u32[]{:S(2)}) %collective-permute-start.42) | collective-permute-done | bytes 8224 | tf_op jit(solution)/shard_map/ppermute | solution.py:277
  141.1 1.0 shard_map.132
  (44 shorter events, 1.4 us)
Async XLA Ops:
  1.4 1.3 collective-permute-start
  2.8 8.0 %copy-start = (s32[2,32]{1,0:T(2,128)S(1)}, s32[2,32]{1,0:T(2,128)}, u32[]{:S(2)}) copy-start(s32[2,32]{1,0:T(2,128)} %counts.1) | copy-start | bytes 772
  2.8 9.7 %collective-permute-start.6 = (bf16[96,256]{1,0:T(8,128)(2,1)S(1)}, bf16[96,256]{1,0:T(8,128)(2,1)S(1)}, u32[]{:S(2)}, u32[]{:S(2)}) collective-permute-start(bf16[96,256]{1,0:T(8,128)(2,1)S(1)} %get-tuple-element.74), channel_id=1, source_target_pairs={{0,6},{1,3},{2,4},{3,1},{4,2},{5,7},{6,0},{7,5},{8,14},{9,11},{10,... | collective-permute-start | bytes 147464 | tf_op jit(solution)/shard_map/ppermute | solution.py:52
  8.3 8.5 %collective-permute-start.5 = (bf16[96,256]{1,0:T(8,128)(2,1)S(1)}, bf16[96,256]{1,0:T(8,128)(2,1)S(1)}, u32[]{:S(2)}, u32[]{:S(2)}) collective-permute-start(bf16[96,256]{1,0:T(8,128)(2,1)S(1)} %get-tuple-element.74), channel_id=1, source_target_pairs={{0,4},{1,5},{2,6},{3,7},{4,0},{5,1},{6,2},{7,3},{8,12},{9,13},{10,... | collective-permute-start | bytes 147464 | tf_op jit(solution)/shard_map/ppermute | solution.py:52
  9.7 7.1 %collective-permute-start.4 = (bf16[96,256]{1,0:T(8,128)(2,1)S(1)}, bf16[96,256]{1,0:T(8,128)(2,1)S(1)}, u32[]{:S(2)}, u32[]{:S(2)}) collective-permute-start(bf16[96,256]{1,0:T(8,128)(2,1)S(1)} %get-tuple-element.74), channel_id=1, source_target_pairs={{0,2},{1,7},{2,0},{3,5},{4,6},{5,3},{6,4},{7,1},{8,10},{9,15},{10,... | collective-permute-start | bytes 147464 | tf_op jit(solution)/shard_map/ppermute | solution.py:52
  12.3 16.6 %collective-permute-start.3 = (bf16[2,256,256]{2,1,0:T(8,128)(2,1)S(1)}, bf16[2,256,256]{2,1,0:T(8,128)(2,1)S(1)}, u32[]{:S(2)}, u32[]{:S(2)}) collective-permute-start(bf16[2,256,256]{2,1,0:T(8,128)(2,1)S(1)} %get-tuple-element.73), channel_id=1, source_target_pairs={{0,1},{1,0},{2,3},{3,2},{4,5},{5,4},{6,7},{7,6},{8,9},{9,8},{10,11... | collective-permute-start | bytes 786440 | tf_op jit(solution)/shard_map/ppermute | solution.py:281
  16.8 12.1 %collective-permute-start.9 = (bf16[4,96,256]{2,1,0:T(8,128)(2,1)S(1)}, bf16[4,96,256]{2,1,0:T(8,128)(2,1)S(1)}, u32[]{:S(2)}, u32[]{:S(2)}) collective-permute-start(bf16[4,96,256]{2,1,0:T(8,128)(2,1)S(1)} %pad_maximum_fusion.s0), channel_id=1, source_target_pairs={{0,24},{1,9},{8,16},{9,1},{16,8},{17,25},{24,0},{25,17},{2,26},{3,... | collective-permute-start | bytes 589832 | tf_op jit(solution)/shard_map/ppermute | solution.py:52
  19.7 9.2 %collective-permute-start.8 = (bf16[4,96,256]{2,1,0:T(8,128)(2,1)S(1)}, bf16[4,96,256]{2,1,0:T(8,128)(2,1)S(1)}, u32[]{:S(2)}, u32[]{:S(2)}) collective-permute-start(bf16[4,96,256]{2,1,0:T(8,128)(2,1)S(1)} %pad_maximum_fusion.s0), channel_id=1, source_target_pairs={{0,16},{1,17},{8,24},{9,25},{16,0},{17,1},{24,8},{25,9},{2,18},{3,... | collective-permute-start | bytes 589832 | tf_op jit(solution)/shard_map/ppermute | solution.py:52
  20.5 8.4 %collective-permute-start.7 = (bf16[4,96,256]{2,1,0:T(8,128)(2,1)S(1)}, bf16[4,96,256]{2,1,0:T(8,128)(2,1)S(1)}, u32[]{:S(2)}, u32[]{:S(2)}) collective-permute-start(bf16[4,96,256]{2,1,0:T(8,128)(2,1)S(1)} %pad_maximum_fusion.s0), channel_id=1, source_target_pairs={{0,8},{1,25},{8,0},{9,17},{16,24},{17,9},{24,16},{25,1},{2,10},{3,... | collective-permute-start | bytes 589832 | tf_op jit(solution)/shard_map/ppermute | solution.py:52
  30.2 6.0 %collective-permute-start.10 = (bf16[4,96,256]{2,1,0:T(8,128)(2,1)S(1)}, bf16[4,96,256]{2,1,0:T(8,128)(2,1)S(1)}, u32[]{:S(2)}, u32[]{:S(2)}) collective-permute-start(bf16[4,96,256]{2,1,0:T(8,128)(2,1)S(1)} %get-tuple-element.76), channel_id=1, source_target_pairs={{0,8},{1,25},{8,0},{9,17},{16,24},{17,9},{24,16},{25,1},{2,10},{3,... | collective-permute-start | bytes 589832 | tf_op jit(solution)/shard_map/ppermute | solution.py:52
  31.1 13.5 %collective-permute-start.11 = (bf16[4,96,256]{2,1,0:T(8,128)(2,1)S(1)}, bf16[4,96,256]{2,1,0:T(8,128)(2,1)S(1)}, u32[]{:S(2)}, u32[]{:S(2)}) collective-permute-start(bf16[4,96,256]{2,1,0:T(8,128)(2,1)S(1)} %get-tuple-element.77), channel_id=1, source_target_pairs={{0,16},{1,17},{8,24},{9,25},{16,0},{17,1},{24,8},{25,9},{2,18},{3,... | collective-permute-start | bytes 589832 | tf_op jit(solution)/shard_map/ppermute | solution.py:52
  35.5 9.9 %collective-permute-start.12 = (bf16[4,96,256]{2,1,0:T(8,128)(2,1)S(1)}, bf16[4,96,256]{2,1,0:T(8,128)(2,1)S(1)}, u32[]{:S(2)}, u32[]{:S(2)}) collective-permute-start(bf16[4,96,256]{2,1,0:T(8,128)(2,1)S(1)} %get-tuple-element.78), channel_id=1, source_target_pairs={{0,24},{1,9},{8,16},{9,1},{16,8},{17,25},{24,0},{25,17},{2,26},{3,... | collective-permute-start | bytes 589832 | tf_op jit(solution)/shard_map/ppermute | solution.py:52
  45.5 6.6 %collective-permute-start.13 = (bf16[96,256]{1,0:T(8,128)(2,1)S(1)}, bf16[96,256]{1,0:T(8,128)(2,1)S(1)}, u32[]{:S(2)}, u32[]{:S(2)}) collective-permute-start(bf16[96,256]{1,0:T(8,128)(2,1)S(1)} %get-tuple-element.80), channel_id=1, source_target_pairs={{0,2},{1,7},{2,0},{3,5},{4,6},{5,3},{6,4},{7,1},{8,10},{9,15},{10,... | collective-permute-start | bytes 147464 | tf_op jit(solution)/shard_map/ppermute | solution.py:52
  46.4 8.2 %collective-permute-start.14 = (bf16[96,256]{1,0:T(8,128)(2,1)S(1)}, bf16[96,256]{1,0:T(8,128)(2,1)S(1)}, u32[]{:S(2)}, u32[]{:S(2)}) collective-permute-start(bf16[96,256]{1,0:T(8,128)(2,1)S(1)} %get-tuple-element.81), channel_id=1, source_target_pairs={{0,4},{1,5},{2,6},{3,7},{4,0},{5,1},{6,2},{7,3},{8,12},{9,13},{10,... | collective-permute-start | bytes 147464 | tf_op jit(solution)/shard_map/ppermute | solution.py:52
  49.3 7.3 %collective-permute-start.15 = (bf16[96,256]{1,0:T(8,128)(2,1)S(1)}, bf16[96,256]{1,0:T(8,128)(2,1)S(1)}, u32[]{:S(2)}, u32[]{:S(2)}) collective-permute-start(bf16[96,256]{1,0:T(8,128)(2,1)S(1)} %get-tuple-element.82), channel_id=1, source_target_pairs={{0,6},{1,3},{2,4},{3,1},{4,2},{5,7},{6,0},{7,5},{8,14},{9,11},{10,... | collective-permute-start | bytes 147464 | tf_op jit(solution)/shard_map/ppermute | solution.py:52
  56.8 6.6 %collective-permute-start.18 = (bf16[96,256]{1,0:T(8,128)(2,1)S(1)}, bf16[96,256]{1,0:T(8,128)(2,1)S(1)}, u32[]{:S(2)}, u32[]{:S(2)}) collective-permute-start(bf16[96,256]{1,0:T(8,128)(2,1)S(1)} %get-tuple-element.83), channel_id=1, source_target_pairs={{0,6},{1,3},{2,4},{3,1},{4,2},{5,7},{6,0},{7,5},{8,14},{9,11},{10,... | collective-permute-start | bytes 147464 | tf_op jit(solution)/shard_map/ppermute | solution.py:52
  58.6 8.5 %collective-permute-start.17 = (bf16[96,256]{1,0:T(8,128)(2,1)S(1)}, bf16[96,256]{1,0:T(8,128)(2,1)S(1)}, u32[]{:S(2)}, u32[]{:S(2)}) collective-permute-start(bf16[96,256]{1,0:T(8,128)(2,1)S(1)} %get-tuple-element.83), channel_id=1, source_target_pairs={{0,4},{1,5},{2,6},{3,7},{4,0},{5,1},{6,2},{7,3},{8,12},{9,13},{10,... | collective-permute-start | bytes 147464 | tf_op jit(solution)/shard_map/ppermute | solution.py:52
  61.4 5.7 %collective-permute-start.16 = (bf16[96,256]{1,0:T(8,128)(2,1)S(1)}, bf16[96,256]{1,0:T(8,128)(2,1)S(1)}, u32[]{:S(2)}, u32[]{:S(2)}) collective-permute-start(bf16[96,256]{1,0:T(8,128)(2,1)S(1)} %get-tuple-element.83), channel_id=1, source_target_pairs={{0,2},{1,7},{2,0},{3,5},{4,6},{5,3},{6,4},{7,1},{8,10},{9,15},{10,... | collective-permute-start | bytes 147464 | tf_op jit(solution)/shard_map/ppermute | solution.py:52
  63.3 8.2 %collective-permute-start.2 = (bf16[2,256,256]{2,1,0:T(8,128)(2,1)S(1)}, bf16[2,256,256]{2,1,0:T(8,128)(2,1)S(1)}, u32[]{:S(2)}, u32[]{:S(2)}) collective-permute-start(bf16[2,256,256]{2,1,0:T(8,128)(2,1)S(1)} %get-tuple-element.70), channel_id=1, source_target_pairs={{0,1},{1,0},{2,3},{3,2},{4,5},{5,4},{6,7},{7,6},{8,9},{9,8},{10,11... | collective-permute-start | bytes 786440 | tf_op jit(solution)/shard_map/ppermute | solution.py:281
  67.1 11.9 %collective-permute-start.21 = (bf16[4,96,256]{2,1,0:T(8,128)(2,1)S(1)}, bf16[4,96,256]{2,1,0:T(8,128)(2,1)S(1)}, u32[]{:S(2)}, u32[]{:S(2)}) collective-permute-start(bf16[4,96,256]{2,1,0:T(8,128)(2,1)S(1)} %pad_maximum_fusion.1.s0), channel_id=1, source_target_pairs={{0,24},{1,9},{8,16},{9,1},{16,8},{17,25},{24,0},{25,17},{2,26},{3,... | collective-permute-start | bytes 589832 | tf_op jit(solution)/shard_map/ppermute | solution.py:52
  69.0 10.1 %collective-permute-start.20 = (bf16[4,96,256]{2,1,0:T(8,128)(2,1)S(1)}, bf16[4,96,256]{2,1,0:T(8,128)(2,1)S(1)}, u32[]{:S(2)}, u32[]{:S(2)}) collective-permute-start(bf16[4,96,256]{2,1,0:T(8,128)(2,1)S(1)} %pad_maximum_fusion.1.s0), channel_id=1, source_target_pairs={{0,16},{1,17},{8,24},{9,25},{16,0},{17,1},{24,8},{25,9},{2,18},{3,... | collective-permute-start | bytes 589832 | tf_op jit(solution)/shard_map/ppermute | solution.py:52
  69.0 10.1 %collective-permute-start.19 = (bf16[4,96,256]{2,1,0:T(8,128)(2,1)S(1)}, bf16[4,96,256]{2,1,0:T(8,128)(2,1)S(1)}, u32[]{:S(2)}, u32[]{:S(2)}) collective-permute-start(bf16[4,96,256]{2,1,0:T(8,128)(2,1)S(1)} %pad_maximum_fusion.1.s0), channel_id=1, source_target_pairs={{0,8},{1,25},{8,0},{9,17},{16,24},{17,9},{24,16},{25,1},{2,10},{3,... | collective-permute-start | bytes 589832 | tf_op jit(solution)/shard_map/ppermute | solution.py:52
  80.4 7.0 %collective-permute-start.24 = (bf16[4,96,256]{2,1,0:T(8,128)(2,1)S(1)}, bf16[4,96,256]{2,1,0:T(8,128)(2,1)S(1)}, u32[]{:S(2)}, u32[]{:S(2)}) collective-permute-start(bf16[4,96,256]{2,1,0:T(8,128)(2,1)S(1)} %get-tuple-element.93), channel_id=1, source_target_pairs={{0,8},{1,25},{8,0},{9,17},{16,24},{17,9},{24,16},{25,1},{2,10},{3,... | collective-permute-start | bytes 589832 | tf_op jit(solution)/shard_map/ppermute | solution.py:52
  80.5 11.6 %collective-permute-start.25 = (bf16[4,96,256]{2,1,0:T(8,128)(2,1)S(1)}, bf16[4,96,256]{2,1,0:T(8,128)(2,1)S(1)}, u32[]{:S(2)}, u32[]{:S(2)}) collective-permute-start(bf16[4,96,256]{2,1,0:T(8,128)(2,1)S(1)} %get-tuple-element.94), channel_id=1, source_target_pairs={{0,16},{1,17},{8,24},{9,25},{16,0},{17,1},{24,8},{25,9},{2,18},{3,... | collective-permute-start | bytes 589832 | tf_op jit(solution)/shard_map/ppermute | solution.py:52
  82.9 9.9 %collective-permute-start.26 = (bf16[4,96,256]{2,1,0:T(8,128)(2,1)S(1)}, bf16[4,96,256]{2,1,0:T(8,128)(2,1)S(1)}, u32[]{:S(2)}, u32[]{:S(2)}) collective-permute-start(bf16[4,96,256]{2,1,0:T(8,128)(2,1)S(1)} %get-tuple-element.95), channel_id=1, source_target_pairs={{0,24},{1,9},{8,16},{9,1},{16,8},{17,25},{24,0},{25,17},{2,26},{3,... | collective-permute-start | bytes 589832 | tf_op jit(solution)/shard_map/ppermute | solution.py:52
  92.8 6.6 %collective-permute-start.27 = (bf16[96,256]{1,0:T(8,128)(2,1)S(1)}, bf16[96,256]{1,0:T(8,128)(2,1)S(1)}, u32[]{:S(2)}, u32[]{:S(2)}) collective-permute-start(bf16[96,256]{1,0:T(8,128)(2,1)S(1)} %get-tuple-element.97), channel_id=1, source_target_pairs={{0,2},{1,7},{2,0},{3,5},{4,6},{5,3},{6,4},{7,1},{8,10},{9,15},{10,... | collective-permute-start | bytes 147464 | tf_op jit(solution)/shard_map/ppermute | solution.py:52
  93.9 8.2 %collective-permute-start.28 = (bf16[96,256]{1,0:T(8,128)(2,1)S(1)}, bf16[96,256]{1,0:T(8,128)(2,1)S(1)}, u32[]{:S(2)}, u32[]{:S(2)}) collective-permute-start(bf16[96,256]{1,0:T(8,128)(2,1)S(1)} %get-tuple-element.98), channel_id=1, source_target_pairs={{0,4},{1,5},{2,6},{3,7},{4,0},{5,1},{6,2},{7,3},{8,12},{9,13},{10,... | collective-permute-start | bytes 147464 | tf_op jit(solution)/shard_map/ppermute | solution.py:52
  97.0 6.2 %collective-permute-start.29 = (bf16[96,256]{1,0:T(8,128)(2,1)S(1)}, bf16[96,256]{1,0:T(8,128)(2,1)S(1)}, u32[]{:S(2)}, u32[]{:S(2)}) collective-permute-start(bf16[96,256]{1,0:T(8,128)(2,1)S(1)} %get-tuple-element.99), channel_id=1, source_target_pairs={{0,6},{1,3},{2,4},{3,1},{4,2},{5,7},{6,0},{7,5},{8,14},{9,11},{10,... | collective-permute-start | bytes 147464 | tf_op jit(solution)/shard_map/ppermute | solution.py:52
  103.5 6.6 %collective-permute-start.32 = (bf16[96,256]{1,0:T(8,128)(2,1)S(1)}, bf16[96,256]{1,0:T(8,128)(2,1)S(1)}, u32[]{:S(2)}, u32[]{:S(2)}) collective-permute-start(bf16[96,256]{1,0:T(8,128)(2,1)S(1)} %get-tuple-element.100), channel_id=1, source_target_pairs={{0,6},{1,3},{2,4},{3,1},{4,2},{5,7},{6,0},{7,5},{8,14},{9,11},{10,... | collective-permute-start | bytes 147464 | tf_op jit(solution)/shard_map/ppermute | solution.py:52
  106.3 8.0 %collective-permute-start.31 = (bf16[96,256]{1,0:T(8,128)(2,1)S(1)}, bf16[96,256]{1,0:T(8,128)(2,1)S(1)}, u32[]{:S(2)}, u32[]{:S(2)}) collective-permute-start(bf16[96,256]{1,0:T(8,128)(2,1)S(1)} %get-tuple-element.100), channel_id=1, source_target_pairs={{0,4},{1,5},{2,6},{3,7},{4,0},{5,1},{6,2},{7,3},{8,12},{9,13},{10,... | collective-permute-start | bytes 147464 | tf_op jit(solution)/shard_map/ppermute | solution.py:52
  109.1 5.5 %collective-permute-start.30 = (bf16[96,256]{1,0:T(8,128)(2,1)S(1)}, bf16[96,256]{1,0:T(8,128)(2,1)S(1)}, u32[]{:S(2)}, u32[]{:S(2)}) collective-permute-start(bf16[96,256]{1,0:T(8,128)(2,1)S(1)} %get-tuple-element.100), channel_id=1, source_target_pairs={{0,2},{1,7},{2,0},{3,5},{4,6},{5,3},{6,4},{7,1},{8,10},{9,15},{10,... | collective-permute-start | bytes 147464 | tf_op jit(solution)/shard_map/ppermute | solution.py:52
  114.7 12.1 %collective-permute-start.36 = (bf16[4,96,256]{2,1,0:T(8,128)(2,1)S(1)}, bf16[4,96,256]{2,1,0:T(8,128)(2,1)S(1)}, u32[]{:S(2)}, u32[]{:S(2)}) collective-permute-start(bf16[4,96,256]{2,1,0:T(8,128)(2,1)S(1)} %pad_maximum_fusion.2.refs_0_), channel_id=1, source_target_pairs={{0,24},{1,9},{8,16},{9,1},{16,8},{17,25},{24,0},{25,17},{2,26},{3,... | collective-permute-start | bytes 589832 | tf_op jit(solution)/shard_map/ppermute | solution.py:52
  116.8 10.0 %collective-permute-start.35 = (bf16[4,96,256]{2,1,0:T(8,128)(2,1)S(1)}, bf16[4,96,256]{2,1,0:T(8,128)(2,1)S(1)}, u32[]{:S(2)}, u32[]{:S(2)}) collective-permute-start(bf16[4,96,256]{2,1,0:T(8,128)(2,1)S(1)} %pad_maximum_fusion.2.refs_0_), channel_id=1, source_target_pairs={{0,16},{1,17},{8,24},{9,25},{16,0},{17,1},{24,8},{25,9},{2,18},{3,... | collective-permute-start | bytes 589832 | tf_op jit(solution)/shard_map/ppermute | solution.py:52
  116.8 10.0 %collective-permute-start.34 = (bf16[4,96,256]{2,1,0:T(8,128)(2,1)S(1)}, bf16[4,96,256]{2,1,0:T(8,128)(2,1)S(1)}, u32[]{:S(2)}, u32[]{:S(2)}) collective-permute-start(bf16[4,96,256]{2,1,0:T(8,128)(2,1)S(1)} %pad_maximum_fusion.2.refs_0_), channel_id=1, source_target_pairs={{0,8},{1,25},{8,0},{9,17},{16,24},{17,9},{24,16},{25,1},{2,10},{3,... | collective-permute-start | bytes 589832 | tf_op jit(solution)/shard_map/ppermute | solution.py:52
  118.8 1.3 collective-permute-start.1
  118.8 3.2 %collective-permute-start.23 = (bf16[256,256]{1,0:T(8,128)(2,1)S(1)}, bf16[256,256]{1,0:T(8,128)(2,1)S(1)}, u32[]{:S(2)}, u32[]{:S(2)}) collective-permute-start(bf16[256,256]{1,0:T(8,128)(2,1)S(1)} %get-tuple-element.90), channel_id=1, source_target_pairs={{0,1},{1,0},{2,3},{3,2},{4,5},{5,4},{6,7},{7,6},{8,9},{9,8},{10,11... | collective-permute-start | bytes 393224 | tf_op jit(solution)/shard_map/ppermute | solution.py:281
  120.2 1.2 collective-permute-start.33
  127.7 1.5 %collective-permute-start.38 = (f32[8,256]{1,0:T(8,128)S(1)}, f32[8,256]{1,0:T(8,128)S(1)}, u32[]{:S(2)}, u32[]{:S(2)}) collective-permute-start(f32[8,256]{1,0:T(8,128)S(1)} %fusion.3), channel_id=1, source_target_pairs={{0,1},{1,0},{2,3},{3,2},{4,5},{5,4},{6,7},{7,6},{8,9},{9,8},{10,11... | collective-permute-start | bytes 24584 | tf_op jit(solution)/shard_map/ppermute | solution.py:281
  129.2 4.9 %collective-permute-start.41 = (f32[8,256]{1,0:T(8,128)S(1)}, f32[8,256]{1,0:T(8,128)S(1)}, u32[]{:S(2)}, u32[]{:S(2)}) collective-permute-start(f32[8,256]{1,0:T(8,128)S(1)} %fusion.2), channel_id=1, source_target_pairs={{0,96},{1,33},{32,64},{33,1},{64,32},{65,97},{96,0},{97,65},{2,98}... | collective-permute-start | bytes 24584 | tf_op jit(solution)/shard_map/ppermute | solution.py:52
  132.2 5.2 %collective-permute-start.40 = (f32[8,256]{1,0:T(8,128)S(1)}, f32[8,256]{1,0:T(8,128)S(1)}, u32[]{:S(2)}, u32[]{:S(2)}) collective-permute-start(f32[8,256]{1,0:T(8,128)S(1)} %fusion.2), channel_id=1, source_target_pairs={{0,64},{1,65},{32,96},{33,97},{64,0},{65,1},{96,32},{97,33},{2,66}... | collective-permute-start | bytes 24584 | tf_op jit(solution)/shard_map/ppermute | solution.py:52
  132.8 4.5 %collective-permute-start.39 = (f32[8,256]{1,0:T(8,128)S(1)}, f32[8,256]{1,0:T(8,128)S(1)}, u32[]{:S(2)}, u32[]{:S(2)}) collective-permute-start(f32[8,256]{1,0:T(8,128)S(1)} %fusion.2), channel_id=1, source_target_pairs={{0,32},{1,97},{32,0},{33,65},{64,96},{65,33},{96,64},{97,1},{2,34}... | collective-permute-start | bytes 24584 | tf_op jit(solution)/shard_map/ppermute | solution.py:52
  133.4 7.7 %collective-permute-start.22 = (bf16[256,256]{1,0:T(8,128)(2,1)S(1)}, bf16[256,256]{1,0:T(8,128)(2,1)S(1)}, u32[]{:S(2)}, u32[]{:S(2)}) collective-permute-start(bf16[256,256]{1,0:T(8,128)(2,1)S(1)} %get-tuple-element.88), channel_id=1, source_target_pairs={{0,1},{1,0},{2,3},{3,2},{4,5},{5,4},{6,7},{7,6},{8,9},{9,8},{10,11... | collective-permute-start | bytes 393224 | tf_op jit(solution)/shard_map/ppermute | solution.py:281
  133.4 7.7 %collective-permute-start.37 = (bf16[256,256]{1,0:T(8,128)(2,1)S(1)}, bf16[256,256]{1,0:T(8,128)(2,1)S(1)}, u32[]{:S(2)}, u32[]{:S(2)}) collective-permute-start(bf16[256,256]{1,0:T(8,128)(2,1)S(1)} %get-tuple-element.108), channel_id=1, source_target_pairs={{0,1},{1,0},{2,3},{3,2},{4,5},{5,4},{6,7},{7,6},{8,9},{9,8},{10,11... | collective-permute-start | bytes 393224 | tf_op jit(solution)/shard_map/ppermute | solution.py:281
  137.4 3.7 %collective-permute-start.42 = (f32[8,256]{1,0:T(8,128)S(1)}, f32[8,256]{1,0:T(8,128)S(1)}, u32[]{:S(2)}, u32[]{:S(2)}) collective-permute-start(f32[8,256]{1,0:T(8,128)S(1)} %add_add_fusion), channel_id=1, source_target_pairs={{0,128},{128,0},{1,129},{129,1},{2,130},{130,2},{3,131},{131,3},{4... | collective-permute-start | bytes 24584 | tf_op jit(solution)/shard_map/ppermute | solution.py:277

commit v2 on v1

--- a/solution.py
+++ b/solution.py
@@ -230,14 +230,16 @@
     else:
         o_own, o_send, sq, g_ref, u_ref, d_ref = refs[4:]
         assemble(refs[:4], g_ref, u_ref, d_ref)
-    for which, (query, out) in enumerate(((q, o_own), (q_other, o_send))):
-        a = mm(query[...], g_ref[...], NT)
-        b = mm(query[...], u_ref[...], NT)
-        hid = (a * jax.nn.sigmoid(a) * b).astype(bf16)
-        o = mm(hid, d_ref[...], NT)
-        out[...] = o.astype(out.dtype)
-        sums = jnp.sum(o * o, axis=-1, keepdims=True)
-        sq[which] = jnp.broadcast_to(sums, (BLK, 128)).T[0:4, :]
+    query = jnp.concatenate([q[...], q_other[...]], axis=0)
+    a = mm(query, g_ref[...], NT)
+    b = mm(query, u_ref[...], NT)
+    hid = (a * jax.nn.sigmoid(a) * b).astype(bf16)
+    o = mm(hid, d_ref[...], NT)
+    o_own[...] = o[0:BLK]
+    o_send[...] = o[BLK:].astype(bf16)
+    sums = jnp.broadcast_to(jnp.sum(o * o, axis=-1, keepdims=True), (2 * BLK, 128)).T
+    sq[0] = sums[0:4, 0:BLK]
+    sq[1] = sums[0:4, BLK:]
 
 
 def apply(q, q_other, weights, assembled):

time: 142 us -> 142 us (level)
  no operation moved by 1% of the time
where the time goes in v2:
time: 142 us
  waiting for transfers between devices  69.1 us (49%)
  starting transfers between devices  62.8 us (44%)
  Pallas kernels  9.07 us (6%)
    ppermute x33, waiting for transfers between devices, shift(): return lax.ppermute(array, (axis, 'core'), pairs)  62.1 us
    ppermute x33, starting transfers between devices, shift(): return lax.ppermute(array, (axis, 'core'), pairs)  61.2 us
    pallas_call x13, Pallas kernels, call(): pl.pallas_call(kernel, in_specs=[SMEM] * len(scalars) + [VMEM] * (len(hel...  9.07 us
    ppermute x1, waiting for transfers between devices, head_sum(): return sq + lax.ppermute(sq, 'hz', SWAP)  3.64 us
    ppermute x9, waiting for transfers between devices, swap(): return lax.ppermute(array, 'core', SWAP)  3.38 us
  transfers between devices with their start and end apart: 43, of which 25 were waited for; matrix products, arithmetic and copies ran while one was open for 0% of the time, Pallas kernels for 2%

profile of v2, /device:TPU:32, one launch (start us, length us, event | category | flops | bytes accessed | tf_op | source)
XLA Modules:
  0.0 141.9 jit_solution(6941018832438580843)
XLA Ops:
  0.6 0.8 shard_map.120
  1.5 1.2 collective-permute-done.recv
  2.8 5.5 %collective-permute-start.6 = (bf16[96,256]{1,0:T(8,128)(2,1)S(1)}, bf16[96,256]{1,0:T(8,128)(2,1)S(1)}, u32[]{:S(2)}, u32[]{:S(2)}) collective-permute-start(bf16[96,256]{1,0:T(8,128)(2,1)S(1)} %get-tuple-element.74), channel_id=1, source_target_pairs={{0,6},{1,3},{2,4},{3,1},{4,2},{5,7},{6,0},{7,5},{8,14},{9,11},{10,... | collective-permute-start | bytes 147464 | tf_op jit(solution)/shard_map/ppermute | solution.py:52
  8.3 1.4 %collective-permute-start.5 = (bf16[96,256]{1,0:T(8,128)(2,1)S(1)}, bf16[96,256]{1,0:T(8,128)(2,1)S(1)}, u32[]{:S(2)}, u32[]{:S(2)}) collective-permute-start(bf16[96,256]{1,0:T(8,128)(2,1)S(1)} %get-tuple-element.74), channel_id=1, source_target_pairs={{0,4},{1,5},{2,6},{3,7},{4,0},{5,1},{6,2},{7,3},{8,12},{9,13},{10,... | collective-permute-start | bytes 147464 | tf_op jit(solution)/shard_map/ppermute | solution.py:52
  9.7 1.0 collective-permute-start.4
  10.7 1.6 %shard_map.122 = (bf16[2,256,256]{2,1,0:T(8,128)(2,1)S(1)}, bf16[2,256,256]{2,1,0:T(8,128)(2,1)S(1)}, bf16[256,256]{1,0:T(8,128)(2,1)S(1)}, bf16[256,256]{1,0:T(...) custom-call(s32[2,32]{1,0:T(2,128)S(1)} %copy-done, ...), custom_call_target="tpu_custom_call" | custom-call | tf_op jit(solution)/shard_map/pallas_call | solution.py:34
  12.5 4.3 %collective-permute-done.5 = bf16[96,256]{1,0:T(8,128)(2,1)S(1)} collective-permute-done((bf16[96,256]{1,0:T(8,128)(2,1)S(1)}, bf16[96,256]{1,0:T(8,128)(2,1)S(1)}, u32[]{:S(2)}, u32[]{:S(2)}) %collective-permute-start.5) | collective-permute-done | bytes 49184 | tf_op jit(solution)/shard_map/ppermute | solution.py:52
  16.8 2.8 %collective-permute-start.9 = (bf16[4,96,256]{2,1,0:T(8,128)(2,1)S(1)}, bf16[4,96,256]{2,1,0:T(8,128)(2,1)S(1)}, u32[]{:S(2)}, u32[]{:S(2)}) collective-permute-start(bf16[4,96,256]{2,1,0:T(8,128)(2,1)S(1)} %pad_maximum_fusion.s0), channel_id=1, source_target_pairs={{0,24},{1,9},{8,16},{9,1},{16,8},{17,25},{24,0},{25,17},{2,26},{3,... | collective-permute-start | bytes 589832 | tf_op jit(solution)/shard_map/ppermute | solution.py:52
  19.7 0.8 collective-permute-start.8
  20.5 0.5 collective-permute-start.7
  21.0 7.9 %collective-permute-done.9.s3 = bf16[4,96,256]{2,1,0:T(8,128)(2,1)S(1)} collective-permute-done((bf16[4,96,256]{2,1,0:T(8,128)(2,1)S(1)}, bf16[4,96,256]{2,1,0:T(8,128)(2,1)S(1)}, u32[]{:S(2)}, u32[]{:S(2)}) %collective-permute-start.9) | collective-permute-done | bytes 196640 | tf_op jit(solution)/shard_map/ppermute | solution.py:52
  28.9 1.3 shard_map.123
  30.2 0.9 collective-permute-start.10
  31.1 4.4 %collective-permute-start.11 = (bf16[4,96,256]{2,1,0:T(8,128)(2,1)S(1)}, bf16[4,96,256]{2,1,0:T(8,128)(2,1)S(1)}, u32[]{:S(2)}, u32[]{:S(2)}) collective-permute-start(bf16[4,96,256]{2,1,0:T(8,128)(2,1)S(1)} %get-tuple-element.77), channel_id=1, source_target_pairs={{0,16},{1,17},{8,24},{9,25},{16,0},{17,1},{24,8},{25,9},{2,18},{3,... | collective-permute-start | bytes 589832 | tf_op jit(solution)/shard_map/ppermute | solution.py:52
  35.5 0.7 collective-permute-done.10.r1
  36.2 8.3 %collective-permute-done.11.r2 = bf16[4,96,256]{2,1,0:T(8,128)(2,1)S(1)} collective-permute-done((bf16[4,96,256]{2,1,0:T(8,128)(2,1)S(1)}, bf16[4,96,256]{2,1,0:T(8,128)(2,1)S(1)}, u32[]{:S(2)}, u32[]{:S(2)}) %collective-permute-start.11) | collective-permute-done | bytes 196640 | tf_op jit(solution)/shard_map/ppermute | solution.py:52
  44.5 0.9 collective-permute-done.12.r3
  45.5 0.9 collective-permute-start.13
  46.4 2.9 %collective-permute-start.14 = (bf16[96,256]{1,0:T(8,128)(2,1)S(1)}, bf16[96,256]{1,0:T(8,128)(2,1)S(1)}, u32[]{:S(2)}, u32[]{:S(2)}) collective-permute-start(bf16[96,256]{1,0:T(8,128)(2,1)S(1)} %get-tuple-element.81), channel_id=1, source_target_pairs={{0,4},{1,5},{2,6},{3,7},{4,0},{5,1},{6,2},{7,3},{8,12},{9,13},{10,... | collective-permute-start | bytes 147464 | tf_op jit(solution)/shard_map/ppermute | solution.py:52
  49.3 2.8 %collective-permute-start.15 = (bf16[96,256]{1,0:T(8,128)(2,1)S(1)}, bf16[96,256]{1,0:T(8,128)(2,1)S(1)}, u32[]{:S(2)}, u32[]{:S(2)}) collective-permute-start(bf16[96,256]{1,0:T(8,128)(2,1)S(1)} %get-tuple-element.82), channel_id=1, source_target_pairs={{0,6},{1,3},{2,4},{3,1},{4,2},{5,7},{6,0},{7,5},{8,14},{9,11},{10,... | collective-permute-start | bytes 147464 | tf_op jit(solution)/shard_map/ppermute | solution.py:52
  52.1 2.5 %collective-permute-done.14.t2 = bf16[96,256]{1,0:T(8,128)(2,1)S(1)} collective-permute-done((bf16[96,256]{1,0:T(8,128)(2,1)S(1)}, bf16[96,256]{1,0:T(8,128)(2,1)S(1)}, u32[]{:S(2)}, u32[]{:S(2)}) %collective-permute-start.14) | collective-permute-done | bytes 49184 | tf_op jit(solution)/shard_map/ppermute | solution.py:52
  54.6 1.9 %collective-permute-done.15.t3 = bf16[96,256]{1,0:T(8,128)(2,1)S(1)} collective-permute-done((bf16[96,256]{1,0:T(8,128)(2,1)S(1)}, bf16[96,256]{1,0:T(8,128)(2,1)S(1)}, u32[]{:S(2)}, u32[]{:S(2)}) %collective-permute-start.15) | collective-permute-done | bytes 49184 | tf_op jit(solution)/shard_map/ppermute | solution.py:52
  56.5 0.2 shard_map.125
  56.8 1.8 %collective-permute-start.18 = (bf16[96,256]{1,0:T(8,128)(2,1)S(1)}, bf16[96,256]{1,0:T(8,128)(2,1)S(1)}, u32[]{:S(2)}, u32[]{:S(2)}) collective-permute-start(bf16[96,256]{1,0:T(8,128)(2,1)S(1)} %get-tuple-element.83), channel_id=1, source_target_pairs={{0,6},{1,3},{2,4},{3,1},{4,2},{5,7},{6,0},{7,5},{8,14},{9,11},{10,... | collective-permute-start | bytes 147464 | tf_op jit(solution)/shard_map/ppermute | solution.py:52
  58.6 2.9 %collective-permute-start.17 = (bf16[96,256]{1,0:T(8,128)(2,1)S(1)}, bf16[96,256]{1,0:T(8,128)(2,1)S(1)}, u32[]{:S(2)}, u32[]{:S(2)}) collective-permute-start(bf16[96,256]{1,0:T(8,128)(2,1)S(1)} %get-tuple-element.83), channel_id=1, source_target_pairs={{0,4},{1,5},{2,6},{3,7},{4,0},{5,1},{6,2},{7,3},{8,12},{9,13},{10,... | collective-permute-start | bytes 147464 | tf_op jit(solution)/shard_map/ppermute | solution.py:52
  61.4 1.9 %collective-permute-start.16 = (bf16[96,256]{1,0:T(8,128)(2,1)S(1)}, bf16[96,256]{1,0:T(8,128)(2,1)S(1)}, u32[]{:S(2)}, u32[]{:S(2)}) collective-permute-start(bf16[96,256]{1,0:T(8,128)(2,1)S(1)} %get-tuple-element.83), channel_id=1, source_target_pairs={{0,2},{1,7},{2,0},{3,5},{4,6},{5,3},{6,4},{7,1},{8,10},{9,15},{10,... | collective-permute-start | bytes 147464 | tf_op jit(solution)/shard_map/ppermute | solution.py:52
  63.4 3.7 %collective-permute-done.17 = bf16[96,256]{1,0:T(8,128)(2,1)S(1)} collective-permute-done((bf16[96,256]{1,0:T(8,128)(2,1)S(1)}, bf16[96,256]{1,0:T(8,128)(2,1)S(1)}, u32[]{:S(2)}, u32[]{:S(2)}) %collective-permute-start.17) | collective-permute-done | bytes 49184 | tf_op jit(solution)/shard_map/ppermute | solution.py:52
  67.1 1.8 %collective-permute-start.21 = (bf16[4,96,256]{2,1,0:T(8,128)(2,1)S(1)}, bf16[4,96,256]{2,1,0:T(8,128)(2,1)S(1)}, u32[]{:S(2)}, u32[]{:S(2)}) collective-permute-start(bf16[4,96,256]{2,1,0:T(8,128)(2,1)S(1)} %pad_maximum_fusion.1.s0), channel_id=1, source_target_pairs={{0,24},{1,9},{8,16},{9,1},{16,8},{17,25},{24,0},{25,17},{2,26},{3,... | collective-permute-start | bytes 589832 | tf_op jit(solution)/shard_map/ppermute | solution.py:52
  69.0 2.5 %collective-permute-start.19 = (bf16[4,96,256]{2,1,0:T(8,128)(2,1)S(1)}, bf16[4,96,256]{2,1,0:T(8,128)(2,1)S(1)}, u32[]{:S(2)}, u32[]{:S(2)}) collective-permute-start(bf16[4,96,256]{2,1,0:T(8,128)(2,1)S(1)} %pad_maximum_fusion.1.s0), channel_id=1, source_target_pairs={{0,8},{1,25},{8,0},{9,17},{16,24},{17,9},{24,16},{25,1},{2,10},{3,... | collective-permute-start | bytes 589832 | tf_op jit(solution)/shard_map/ppermute | solution.py:52
  71.5 7.5 %collective-permute-done.21.s3 = bf16[4,96,256]{2,1,0:T(8,128)(2,1)S(1)} collective-permute-done((bf16[4,96,256]{2,1,0:T(8,128)(2,1)S(1)}, bf16[4,96,256]{2,1,0:T(8,128)(2,1)S(1)}, u32[]{:S(2)}, u32[]{:S(2)}) %collective-permute-start.21) | collective-permute-done | bytes 196640 | tf_op jit(solution)/shard_map/ppermute | solution.py:52
  79.1 1.3 shard_map.126
  80.5 2.4 %collective-permute-start.25 = (bf16[4,96,256]{2,1,0:T(8,128)(2,1)S(1)}, bf16[4,96,256]{2,1,0:T(8,128)(2,1)S(1)}, u32[]{:S(2)}, u32[]{:S(2)}) collective-permute-start(bf16[4,96,256]{2,1,0:T(8,128)(2,1)S(1)} %get-tuple-element.94), channel_id=1, source_target_pairs={{0,16},{1,17},{8,24},{9,25},{16,0},{17,1},{24,8},{25,9},{2,18},{3,... | collective-permute-start | bytes 589832 | tf_op jit(solution)/shard_map/ppermute | solution.py:52
  82.9 2.3 %collective-permute-start.26 = (bf16[4,96,256]{2,1,0:T(8,128)(2,1)S(1)}, bf16[4,96,256]{2,1,0:T(8,128)(2,1)S(1)}, u32[]{:S(2)}, u32[]{:S(2)}) collective-permute-start(bf16[4,96,256]{2,1,0:T(8,128)(2,1)S(1)} %get-tuple-element.95), channel_id=1, source_target_pairs={{0,24},{1,9},{8,16},{9,1},{16,8},{17,25},{24,0},{25,17},{2,26},{3,... | collective-permute-start | bytes 589832 | tf_op jit(solution)/shard_map/ppermute | solution.py:52
  85.2 2.2 %collective-permute-done.24.r1 = bf16[4,96,256]{2,1,0:T(8,128)(2,1)S(1)} collective-permute-done((bf16[4,96,256]{2,1,0:T(8,128)(2,1)S(1)}, bf16[4,96,256]{2,1,0:T(8,128)(2,1)S(1)}, u32[]{:S(2)}, u32[]{:S(2)}) %collective-permute-start.24) | collective-permute-done | bytes 196640 | tf_op jit(solution)/shard_map/ppermute | solution.py:52
  87.4 4.6 %collective-permute-done.25.r2 = bf16[4,96,256]{2,1,0:T(8,128)(2,1)S(1)} collective-permute-done((bf16[4,96,256]{2,1,0:T(8,128)(2,1)S(1)}, bf16[4,96,256]{2,1,0:T(8,128)(2,1)S(1)}, u32[]{:S(2)}, u32[]{:S(2)}) %collective-permute-start.25) | collective-permute-done | bytes 196640 | tf_op jit(solution)/shard_map/ppermute | solution.py:52
  92.0 0.7 collective-permute-done.26.r3
  92.8 1.1 collective-permute-start.27
  93.9 3.1 %collective-permute-start.28 = (bf16[96,256]{1,0:T(8,128)(2,1)S(1)}, bf16[96,256]{1,0:T(8,128)(2,1)S(1)}, u32[]{:S(2)}, u32[]{:S(2)}) collective-permute-start(bf16[96,256]{1,0:T(8,128)(2,1)S(1)} %get-tuple-element.98), channel_id=1, source_target_pairs={{0,4},{1,5},{2,6},{3,7},{4,0},{5,1},{6,2},{7,3},{8,12},{9,13},{10,... | collective-permute-start | bytes 147464 | tf_op jit(solution)/shard_map/ppermute | solution.py:52
  97.0 2.4 %collective-permute-start.29 = (bf16[96,256]{1,0:T(8,128)(2,1)S(1)}, bf16[96,256]{1,0:T(8,128)(2,1)S(1)}, u32[]{:S(2)}, u32[]{:S(2)}) collective-permute-start(bf16[96,256]{1,0:T(8,128)(2,1)S(1)} %get-tuple-element.99), channel_id=1, source_target_pairs={{0,6},{1,3},{2,4},{3,1},{4,2},{5,7},{6,0},{7,5},{8,14},{9,11},{10,... | collective-permute-start | bytes 147464 | tf_op jit(solution)/shard_map/ppermute | solution.py:52
  99.4 2.7 %collective-permute-done.28.t2 = bf16[96,256]{1,0:T(8,128)(2,1)S(1)} collective-permute-done((bf16[96,256]{1,0:T(8,128)(2,1)S(1)}, bf16[96,256]{1,0:T(8,128)(2,1)S(1)}, u32[]{:S(2)}, u32[]{:S(2)}) %collective-permute-start.28) | collective-permute-done | bytes 49184 | tf_op jit(solution)/shard_map/ppermute | solution.py:52
  102.1 1.1 collective-permute-done.29.t3
  103.3 0.2 shard_map.129
  103.5 2.8 %collective-permute-start.32 = (bf16[96,256]{1,0:T(8,128)(2,1)S(1)}, bf16[96,256]{1,0:T(8,128)(2,1)S(1)}, u32[]{:S(2)}, u32[]{:S(2)}) collective-permute-start(bf16[96,256]{1,0:T(8,128)(2,1)S(1)} %get-tuple-element.100), channel_id=1, source_target_pairs={{0,6},{1,3},{2,4},{3,1},{4,2},{5,7},{6,0},{7,5},{8,14},{9,11},{10,... | collective-permute-start | bytes 147464 | tf_op jit(solution)/shard_map/ppermute | solution.py:52
  106.3 2.8 %collective-permute-start.31 = (bf16[96,256]{1,0:T(8,128)(2,1)S(1)}, bf16[96,256]{1,0:T(8,128)(2,1)S(1)}, u32[]{:S(2)}, u32[]{:S(2)}) collective-permute-start(bf16[96,256]{1,0:T(8,128)(2,1)S(1)} %get-tuple-element.100), channel_id=1, source_target_pairs={{0,4},{1,5},{2,6},{3,7},{4,0},{5,1},{6,2},{7,3},{8,12},{9,13},{10,... | collective-permute-start | bytes 147464 | tf_op jit(solution)/shard_map/ppermute | solution.py:52
  109.1 1.0 collective-permute-start.30
  110.1 4.2 %collective-permute-done.31 = bf16[96,256]{1,0:T(8,128)(2,1)S(1)} collective-permute-done((bf16[96,256]{1,0:T(8,128)(2,1)S(1)}, bf16[96,256]{1,0:T(8,128)(2,1)S(1)}, u32[]{:S(2)}, u32[]{:S(2)}) %collective-permute-start.31) | collective-permute-done | bytes 49184 | tf_op jit(solution)/shard_map/ppermute | solution.py:52
  114.3 0.3 collective-permute-done.30
  114.7 2.1 %collective-permute-start.36 = (bf16[4,96,256]{2,1,0:T(8,128)(2,1)S(1)}, bf16[4,96,256]{2,1,0:T(8,128)(2,1)S(1)}, u32[]{:S(2)}, u32[]{:S(2)}) collective-permute-start(bf16[4,96,256]{2,1,0:T(8,128)(2,1)S(1)} %pad_maximum_fusion.2.refs_0_), channel_id=1, source_target_pairs={{0,24},{1,9},{8,16},{9,1},{16,8},{17,25},{24,0},{25,17},{2,26},{3,... | collective-permute-start | bytes 589832 | tf_op jit(solution)/shard_map/ppermute | solution.py:52
  116.8 2.1 %collective-permute-start.34 = (bf16[4,96,256]{2,1,0:T(8,128)(2,1)S(1)}, bf16[4,96,256]{2,1,0:T(8,128)(2,1)S(1)}, u32[]{:S(2)}, u32[]{:S(2)}) collective-permute-start(bf16[4,96,256]{2,1,0:T(8,128)(2,1)S(1)} %pad_maximum_fusion.2.refs_0_), channel_id=1, source_target_pairs={{0,8},{1,25},{8,0},{9,17},{16,24},{17,9},{24,16},{25,1},{2,10},{3,... | collective-permute-start | bytes 589832 | tf_op jit(solution)/shard_map/ppermute | solution.py:52
  118.8 0.5 collective-permute-start.23
  119.4 0.8 collective-permute-done.1.q_other
  120.3 0.9 shard_map.127
  121.4 0.6 shard_map.130
  122.1 4.7 %collective-permute-done.36.refs_3_ = bf16[4,96,256]{2,1,0:T(8,128)(2,1)S(1)} collective-permute-done((bf16[4,96,256]{2,1,0:T(8,128)(2,1)S(1)}, bf16[4,96,256]{2,1,0:T(8,128)(2,1)S(1)}, u32[]{:S(2)}, u32[]{:S(2)}) %collective-permute-start.36) | collective-permute-done | bytes 196640 | tf_op jit(solution)/shard_map/ppermute | solution.py:52
  126.8 0.9 shard_map.131
  127.9 1.1 collective-permute-done.38
  129.0 3.0 %collective-permute-start.41 = (f32[8,256]{1,0:T(8,128)S(1)}, f32[8,256]{1,0:T(8,128)S(1)}, u32[]{:S(2)}, u32[]{:S(2)}) collective-permute-start(f32[8,256]{1,0:T(8,128)S(1)} %fusion.2), channel_id=1, source_target_pairs={{0,96},{1,33},{32,64},{33,1},{64,32},{65,97},{96,0},{97,65},{2,98}... | collective-permute-start | bytes 24584 | tf_op jit(solution)/shard_map/ppermute | solution.py:52
  132.0 0.6 collective-permute-start.40
  132.6 0.6 collective-permute-start.39
  133.2 0.5 collective-permute-start.37
  133.7 0.3 collective-permute-done.41
  134.0 3.2 %collective-permute-done.40 = f32[8,256]{1,0:T(8,128)S(1)} collective-permute-done((f32[8,256]{1,0:T(8,128)S(1)}, f32[8,256]{1,0:T(8,128)S(1)}, u32[]{:S(2)}, u32[]{:S(2)}) %collective-permute-start.40) | collective-permute-done | bytes 8224 | tf_op jit(solution)/shard_map/ppermute | solution.py:52
  137.3 3.6 %collective-permute-done.42 = f32[8,256]{1,0:T(8,128)S(1)} collective-permute-done((f32[8,256]{1,0:T(8,128)S(1)}, f32[8,256]{1,0:T(8,128)S(1)}, u32[]{:S(2)}, u32[]{:S(2)}) %collective-permute-start.42) | collective-permute-done | bytes 8224 | tf_op jit(solution)/shard_map/ppermute | solution.py:279
  140.9 1.0 shard_map.132
  (44 shorter events, 1.3 us)
Async XLA Ops:
  1.4 1.3 collective-permute-start
  2.8 8.0 %copy-start = (s32[2,32]{1,0:T(2,128)S(1)}, s32[2,32]{1,0:T(2,128)}, u32[]{:S(2)}) copy-start(s32[2,32]{1,0:T(2,128)} %counts.1) | copy-start | bytes 772
  2.8 9.7 %collective-permute-start.6 = (bf16[96,256]{1,0:T(8,128)(2,1)S(1)}, bf16[96,256]{1,0:T(8,128)(2,1)S(1)}, u32[]{:S(2)}, u32[]{:S(2)}) collective-permute-start(bf16[96,256]{1,0:T(8,128)(2,1)S(1)} %get-tuple-element.74), channel_id=1, source_target_pairs={{0,6},{1,3},{2,4},{3,1},{4,2},{5,7},{6,0},{7,5},{8,14},{9,11},{10,... | collective-permute-start | bytes 147464 | tf_op jit(solution)/shard_map/ppermute | solution.py:52
  8.3 8.5 %collective-permute-start.5 = (bf16[96,256]{1,0:T(8,128)(2,1)S(1)}, bf16[96,256]{1,0:T(8,128)(2,1)S(1)}, u32[]{:S(2)}, u32[]{:S(2)}) collective-permute-start(bf16[96,256]{1,0:T(8,128)(2,1)S(1)} %get-tuple-element.74), channel_id=1, source_target_pairs={{0,4},{1,5},{2,6},{3,7},{4,0},{5,1},{6,2},{7,3},{8,12},{9,13},{10,... | collective-permute-start | bytes 147464 | tf_op jit(solution)/shard_map/ppermute | solution.py:52
  9.7 7.1 %collective-permute-start.4 = (bf16[96,256]{1,0:T(8,128)(2,1)S(1)}, bf16[96,256]{1,0:T(8,128)(2,1)S(1)}, u32[]{:S(2)}, u32[]{:S(2)}) collective-permute-start(bf16[96,256]{1,0:T(8,128)(2,1)S(1)} %get-tuple-element.74), channel_id=1, source_target_pairs={{0,2},{1,7},{2,0},{3,5},{4,6},{5,3},{6,4},{7,1},{8,10},{9,15},{10,... | collective-permute-start | bytes 147464 | tf_op jit(solution)/shard_map/ppermute | solution.py:52
  12.3 16.6 %collective-permute-start.3 = (bf16[2,256,256]{2,1,0:T(8,128)(2,1)S(1)}, bf16[2,256,256]{2,1,0:T(8,128)(2,1)S(1)}, u32[]{:S(2)}, u32[]{:S(2)}) collective-permute-start(bf16[2,256,256]{2,1,0:T(8,128)(2,1)S(1)} %get-tuple-element.73), channel_id=1, source_target_pairs={{0,1},{1,0},{2,3},{3,2},{4,5},{5,4},{6,7},{7,6},{8,9},{9,8},{10,11... | collective-permute-start | bytes 786440 | tf_op jit(solution)/shard_map/ppermute | solution.py:283
  16.8 12.1 %collective-permute-start.9 = (bf16[4,96,256]{2,1,0:T(8,128)(2,1)S(1)}, bf16[4,96,256]{2,1,0:T(8,128)(2,1)S(1)}, u32[]{:S(2)}, u32[]{:S(2)}) collective-permute-start(bf16[4,96,256]{2,1,0:T(8,128)(2,1)S(1)} %pad_maximum_fusion.s0), channel_id=1, source_target_pairs={{0,24},{1,9},{8,16},{9,1},{16,8},{17,25},{24,0},{25,17},{2,26},{3,... | collective-permute-start | bytes 589832 | tf_op jit(solution)/shard_map/ppermute | solution.py:52
  19.7 9.2 %collective-permute-start.8 = (bf16[4,96,256]{2,1,0:T(8,128)(2,1)S(1)}, bf16[4,96,256]{2,1,0:T(8,128)(2,1)S(1)}, u32[]{:S(2)}, u32[]{:S(2)}) collective-permute-start(bf16[4,96,256]{2,1,0:T(8,128)(2,1)S(1)} %pad_maximum_fusion.s0), channel_id=1, source_target_pairs={{0,16},{1,17},{8,24},{9,25},{16,0},{17,1},{24,8},{25,9},{2,18},{3,... | collective-permute-start | bytes 589832 | tf_op jit(solution)/shard_map/ppermute | solution.py:52
  20.5 8.4 %collective-permute-start.7 = (bf16[4,96,256]{2,1,0:T(8,128)(2,1)S(1)}, bf16[4,96,256]{2,1,0:T(8,128)(2,1)S(1)}, u32[]{:S(2)}, u32[]{:S(2)}) collective-permute-start(bf16[4,96,256]{2,1,0:T(8,128)(2,1)S(1)} %pad_maximum_fusion.s0), channel_id=1, source_target_pairs={{0,8},{1,25},{8,0},{9,17},{16,24},{17,9},{24,16},{25,1},{2,10},{3,... | collective-permute-start | bytes 589832 | tf_op jit(solution)/shard_map/ppermute | solution.py:52
  30.2 6.0 %collective-permute-start.10 = (bf16[4,96,256]{2,1,0:T(8,128)(2,1)S(1)}, bf16[4,96,256]{2,1,0:T(8,128)(2,1)S(1)}, u32[]{:S(2)}, u32[]{:S(2)}) collective-permute-start(bf16[4,96,256]{2,1,0:T(8,128)(2,1)S(1)} %get-tuple-element.76), channel_id=1, source_target_pairs={{0,8},{1,25},{8,0},{9,17},{16,24},{17,9},{24,16},{25,1},{2,10},{3,... | collective-permute-start | bytes 589832 | tf_op jit(solution)/shard_map/ppermute | solution.py:52
  31.1 13.5 %collective-permute-start.11 = (bf16[4,96,256]{2,1,0:T(8,128)(2,1)S(1)}, bf16[4,96,256]{2,1,0:T(8,128)(2,1)S(1)}, u32[]{:S(2)}, u32[]{:S(2)}) collective-permute-start(bf16[4,96,256]{2,1,0:T(8,128)(2,1)S(1)} %get-tuple-element.77), channel_id=1, source_target_pairs={{0,16},{1,17},{8,24},{9,25},{16,0},{17,1},{24,8},{25,9},{2,18},{3,... | collective-permute-start | bytes 589832 | tf_op jit(solution)/shard_map/ppermute | solution.py:52
  35.5 9.9 %collective-permute-start.12 = (bf16[4,96,256]{2,1,0:T(8,128)(2,1)S(1)}, bf16[4,96,256]{2,1,0:T(8,128)(2,1)S(1)}, u32[]{:S(2)}, u32[]{:S(2)}) collective-permute-start(bf16[4,96,256]{2,1,0:T(8,128)(2,1)S(1)} %get-tuple-element.78), channel_id=1, source_target_pairs={{0,24},{1,9},{8,16},{9,1},{16,8},{17,25},{24,0},{25,17},{2,26},{3,... | collective-permute-start | bytes 589832 | tf_op jit(solution)/shard_map/ppermute | solution.py:52
  45.5 6.6 %collective-permute-start.13 = (bf16[96,256]{1,0:T(8,128)(2,1)S(1)}, bf16[96,256]{1,0:T(8,128)(2,1)S(1)}, u32[]{:S(2)}, u32[]{:S(2)}) collective-permute-start(bf16[96,256]{1,0:T(8,128)(2,1)S(1)} %get-tuple-element.80), channel_id=1, source_target_pairs={{0,2},{1,7},{2,0},{3,5},{4,6},{5,3},{6,4},{7,1},{8,10},{9,15},{10,... | collective-permute-start | bytes 147464 | tf_op jit(solution)/shard_map/ppermute | solution.py:52
  46.4 8.2 %collective-permute-start.14 = (bf16[96,256]{1,0:T(8,128)(2,1)S(1)}, bf16[96,256]{1,0:T(8,128)(2,1)S(1)}, u32[]{:S(2)}, u32[]{:S(2)}) collective-permute-start(bf16[96,256]{1,0:T(8,128)(2,1)S(1)} %get-tuple-element.81), channel_id=1, source_target_pairs={{0,4},{1,5},{2,6},{3,7},{4,0},{5,1},{6,2},{7,3},{8,12},{9,13},{10,... | collective-permute-start | bytes 147464 | tf_op jit(solution)/shard_map/ppermute | solution.py:52
  49.3 7.3 %collective-permute-start.15 = (bf16[96,256]{1,0:T(8,128)(2,1)S(1)}, bf16[96,256]{1,0:T(8,128)(2,1)S(1)}, u32[]{:S(2)}, u32[]{:S(2)}) collective-permute-start(bf16[96,256]{1,0:T(8,128)(2,1)S(1)} %get-tuple-element.82), channel_id=1, source_target_pairs={{0,6},{1,3},{2,4},{3,1},{4,2},{5,7},{6,0},{7,5},{8,14},{9,11},{10,... | collective-permute-start | bytes 147464 | tf_op jit(solution)/shard_map/ppermute | solution.py:52
  56.8 6.6 %collective-permute-start.18 = (bf16[96,256]{1,0:T(8,128)(2,1)S(1)}, bf16[96,256]{1,0:T(8,128)(2,1)S(1)}, u32[]{:S(2)}, u32[]{:S(2)}) collective-permute-start(bf16[96,256]{1,0:T(8,128)(2,1)S(1)} %get-tuple-element.83), channel_id=1, source_target_pairs={{0,6},{1,3},{2,4},{3,1},{4,2},{5,7},{6,0},{7,5},{8,14},{9,11},{10,... | collective-permute-start | bytes 147464 | tf_op jit(solution)/shard_map/ppermute | solution.py:52
  58.6 8.5 %collective-permute-start.17 = (bf16[96,256]{1,0:T(8,128)(2,1)S(1)}, bf16[96,256]{1,0:T(8,128)(2,1)S(1)}, u32[]{:S(2)}, u32[]{:S(2)}) collective-permute-start(bf16[96,256]{1,0:T(8,128)(2,1)S(1)} %get-tuple-element.83), channel_id=1, source_target_pairs={{0,4},{1,5},{2,6},{3,7},{4,0},{5,1},{6,2},{7,3},{8,12},{9,13},{10,... | collective-permute-start | bytes 147464 | tf_op jit(solution)/shard_map/ppermute | solution.py:52
  61.4 5.7 %collective-permute-start.16 = (bf16[96,256]{1,0:T(8,128)(2,1)S(1)}, bf16[96,256]{1,0:T(8,128)(2,1)S(1)}, u32[]{:S(2)}, u32[]{:S(2)}) collective-permute-start(bf16[96,256]{1,0:T(8,128)(2,1)S(1)} %get-tuple-element.83), channel_id=1, source_target_pairs={{0,2},{1,7},{2,0},{3,5},{4,6},{5,3},{6,4},{7,1},{8,10},{9,15},{10,... | collective-permute-start | bytes 147464 | tf_op jit(solution)/shard_map/ppermute | solution.py:52
  63.3 8.2 %collective-permute-start.2 = (bf16[2,256,256]{2,1,0:T(8,128)(2,1)S(1)}, bf16[2,256,256]{2,1,0:T(8,128)(2,1)S(1)}, u32[]{:S(2)}, u32[]{:S(2)}) collective-permute-start(bf16[2,256,256]{2,1,0:T(8,128)(2,1)S(1)} %get-tuple-element.70), channel_id=1, source_target_pairs={{0,1},{1,0},{2,3},{3,2},{4,5},{5,4},{6,7},{7,6},{8,9},{9,8},{10,11... | collective-permute-start | bytes 786440 | tf_op jit(solution)/shard_map/ppermute | solution.py:283
  67.1 11.9 %collective-permute-start.21 = (bf16[4,96,256]{2,1,0:T(8,128)(2,1)S(1)}, bf16[4,96,256]{2,1,0:T(8,128)(2,1)S(1)}, u32[]{:S(2)}, u32[]{:S(2)}) collective-permute-start(bf16[4,96,256]{2,1,0:T(8,128)(2,1)S(1)} %pad_maximum_fusion.1.s0), channel_id=1, source_target_pairs={{0,24},{1,9},{8,16},{9,1},{16,8},{17,25},{24,0},{25,17},{2,26},{3,... | collective-permute-start | bytes 589832 | tf_op jit(solution)/shard_map/ppermute | solution.py:52
  69.0 10.1 %collective-permute-start.20 = (bf16[4,96,256]{2,1,0:T(8,128)(2,1)S(1)}, bf16[4,96,256]{2,1,0:T(8,128)(2,1)S(1)}, u32[]{:S(2)}, u32[]{:S(2)}) collective-permute-start(bf16[4,96,256]{2,1,0:T(8,128)(2,1)S(1)} %pad_maximum_fusion.1.s0), channel_id=1, source_target_pairs={{0,16},{1,17},{8,24},{9,25},{16,0},{17,1},{24,8},{25,9},{2,18},{3,... | collective-permute-start | bytes 589832 | tf_op jit(solution)/shard_map/ppermute | solution.py:52
  69.0 10.1 %collective-permute-start.19 = (bf16[4,96,256]{2,1,0:T(8,128)(2,1)S(1)}, bf16[4,96,256]{2,1,0:T(8,128)(2,1)S(1)}, u32[]{:S(2)}, u32[]{:S(2)}) collective-permute-start(bf16[4,96,256]{2,1,0:T(8,128)(2,1)S(1)} %pad_maximum_fusion.1.s0), channel_id=1, source_target_pairs={{0,8},{1,25},{8,0},{9,17},{16,24},{17,9},{24,16},{25,1},{2,10},{3,... | collective-permute-start | bytes 589832 | tf_op jit(solution)/shard_map/ppermute | solution.py:52
  80.4 7.0 %collective-permute-start.24 = (bf16[4,96,256]{2,1,0:T(8,128)(2,1)S(1)}, bf16[4,96,256]{2,1,0:T(8,128)(2,1)S(1)}, u32[]{:S(2)}, u32[]{:S(2)}) collective-permute-start(bf16[4,96,256]{2,1,0:T(8,128)(2,1)S(1)} %get-tuple-element.93), channel_id=1, source_target_pairs={{0,8},{1,25},{8,0},{9,17},{16,24},{17,9},{24,16},{25,1},{2,10},{3,... | collective-permute-start | bytes 589832 | tf_op jit(solution)/shard_map/ppermute | solution.py:52
  80.5 11.6 %collective-permute-start.25 = (bf16[4,96,256]{2,1,0:T(8,128)(2,1)S(1)}, bf16[4,96,256]{2,1,0:T(8,128)(2,1)S(1)}, u32[]{:S(2)}, u32[]{:S(2)}) collective-permute-start(bf16[4,96,256]{2,1,0:T(8,128)(2,1)S(1)} %get-tuple-element.94), channel_id=1, source_target_pairs={{0,16},{1,17},{8,24},{9,25},{16,0},{17,1},{24,8},{25,9},{2,18},{3,... | collective-permute-start | bytes 589832 | tf_op jit(solution)/shard_map/ppermute | solution.py:52
  82.9 9.9 %collective-permute-start.26 = (bf16[4,96,256]{2,1,0:T(8,128)(2,1)S(1)}, bf16[4,96,256]{2,1,0:T(8,128)(2,1)S(1)}, u32[]{:S(2)}, u32[]{:S(2)}) collective-permute-start(bf16[4,96,256]{2,1,0:T(8,128)(2,1)S(1)} %get-tuple-element.95), channel_id=1, source_target_pairs={{0,24},{1,9},{8,16},{9,1},{16,8},{17,25},{24,0},{25,17},{2,26},{3,... | collective-permute-start | bytes 589832 | tf_op jit(solution)/shard_map/ppermute | solution.py:52
  92.8 6.6 %collective-permute-start.27 = (bf16[96,256]{1,0:T(8,128)(2,1)S(1)}, bf16[96,256]{1,0:T(8,128)(2,1)S(1)}, u32[]{:S(2)}, u32[]{:S(2)}) collective-permute-start(bf16[96,256]{1,0:T(8,128)(2,1)S(1)} %get-tuple-element.97), channel_id=1, source_target_pairs={{0,2},{1,7},{2,0},{3,5},{4,6},{5,3},{6,4},{7,1},{8,10},{9,15},{10,... | collective-permute-start | bytes 147464 | tf_op jit(solution)/shard_map/ppermute | solution.py:52
  93.9 8.2 %collective-permute-start.28 = (bf16[96,256]{1,0:T(8,128)(2,1)S(1)}, bf16[96,256]{1,0:T(8,128)(2,1)S(1)}, u32[]{:S(2)}, u32[]{:S(2)}) collective-permute-start(bf16[96,256]{1,0:T(8,128)(2,1)S(1)} %get-tuple-element.98), channel_id=1, source_target_pairs={{0,4},{1,5},{2,6},{3,7},{4,0},{5,1},{6,2},{7,3},{8,12},{9,13},{10,... | collective-permute-start | bytes 147464 | tf_op jit(solution)/shard_map/ppermute | solution.py:52
  97.0 6.2 %collective-permute-start.29 = (bf16[96,256]{1,0:T(8,128)(2,1)S(1)}, bf16[96,256]{1,0:T(8,128)(2,1)S(1)}, u32[]{:S(2)}, u32[]{:S(2)}) collective-permute-start(bf16[96,256]{1,0:T(8,128)(2,1)S(1)} %get-tuple-element.99), channel_id=1, source_target_pairs={{0,6},{1,3},{2,4},{3,1},{4,2},{5,7},{6,0},{7,5},{8,14},{9,11},{10,... | collective-permute-start | bytes 147464 | tf_op jit(solution)/shard_map/ppermute | solution.py:52
  103.5 6.6 %collective-permute-start.32 = (bf16[96,256]{1,0:T(8,128)(2,1)S(1)}, bf16[96,256]{1,0:T(8,128)(2,1)S(1)}, u32[]{:S(2)}, u32[]{:S(2)}) collective-permute-start(bf16[96,256]{1,0:T(8,128)(2,1)S(1)} %get-tuple-element.100), channel_id=1, source_target_pairs={{0,6},{1,3},{2,4},{3,1},{4,2},{5,7},{6,0},{7,5},{8,14},{9,11},{10,... | collective-permute-start | bytes 147464 | tf_op jit(solution)/shard_map/ppermute | solution.py:52
  106.3 8.0 %collective-permute-start.31 = (bf16[96,256]{1,0:T(8,128)(2,1)S(1)}, bf16[96,256]{1,0:T(8,128)(2,1)S(1)}, u32[]{:S(2)}, u32[]{:S(2)}) collective-permute-start(bf16[96,256]{1,0:T(8,128)(2,1)S(1)} %get-tuple-element.100), channel_id=1, source_target_pairs={{0,4},{1,5},{2,6},{3,7},{4,0},{5,1},{6,2},{7,3},{8,12},{9,13},{10,... | collective-permute-start | bytes 147464 | tf_op jit(solution)/shard_map/ppermute | solution.py:52
  109.1 5.5 %collective-permute-start.30 = (bf16[96,256]{1,0:T(8,128)(2,1)S(1)}, bf16[96,256]{1,0:T(8,128)(2,1)S(1)}, u32[]{:S(2)}, u32[]{:S(2)}) collective-permute-start(bf16[96,256]{1,0:T(8,128)(2,1)S(1)} %get-tuple-element.100), channel_id=1, source_target_pairs={{0,2},{1,7},{2,0},{3,5},{4,6},{5,3},{6,4},{7,1},{8,10},{9,15},{10,... | collective-permute-start | bytes 147464 | tf_op jit(solution)/shard_map/ppermute | solution.py:52
  114.7 12.1 %collective-permute-start.36 = (bf16[4,96,256]{2,1,0:T(8,128)(2,1)S(1)}, bf16[4,96,256]{2,1,0:T(8,128)(2,1)S(1)}, u32[]{:S(2)}, u32[]{:S(2)}) collective-permute-start(bf16[4,96,256]{2,1,0:T(8,128)(2,1)S(1)} %pad_maximum_fusion.2.refs_0_), channel_id=1, source_target_pairs={{0,24},{1,9},{8,16},{9,1},{16,8},{17,25},{24,0},{25,17},{2,26},{3,... | collective-permute-start | bytes 589832 | tf_op jit(solution)/shard_map/ppermute | solution.py:52
  116.8 10.0 %collective-permute-start.35 = (bf16[4,96,256]{2,1,0:T(8,128)(2,1)S(1)}, bf16[4,96,256]{2,1,0:T(8,128)(2,1)S(1)}, u32[]{:S(2)}, u32[]{:S(2)}) collective-permute-start(bf16[4,96,256]{2,1,0:T(8,128)(2,1)S(1)} %pad_maximum_fusion.2.refs_0_), channel_id=1, source_target_pairs={{0,16},{1,17},{8,24},{9,25},{16,0},{17,1},{24,8},{25,9},{2,18},{3,... | collective-permute-start | bytes 589832 | tf_op jit(solution)/shard_map/ppermute | solution.py:52
  116.8 10.0 %collective-permute-start.34 = (bf16[4,96,256]{2,1,0:T(8,128)(2,1)S(1)}, bf16[4,96,256]{2,1,0:T(8,128)(2,1)S(1)}, u32[]{:S(2)}, u32[]{:S(2)}) collective-permute-start(bf16[4,96,256]{2,1,0:T(8,128)(2,1)S(1)} %pad_maximum_fusion.2.refs_0_), channel_id=1, source_target_pairs={{0,8},{1,25},{8,0},{9,17},{16,24},{17,9},{24,16},{25,1},{2,10},{3,... | collective-permute-start | bytes 589832 | tf_op jit(solution)/shard_map/ppermute | solution.py:52
  118.8 1.3 collective-permute-start.1
  118.8 3.2 %collective-permute-start.23 = (bf16[256,256]{1,0:T(8,128)(2,1)S(1)}, bf16[256,256]{1,0:T(8,128)(2,1)S(1)}, u32[]{:S(2)}, u32[]{:S(2)}) collective-permute-start(bf16[256,256]{1,0:T(8,128)(2,1)S(1)} %get-tuple-element.90), channel_id=1, source_target_pairs={{0,1},{1,0},{2,3},{3,2},{4,5},{5,4},{6,7},{7,6},{8,9},{9,8},{10,11... | collective-permute-start | bytes 393224 | tf_op jit(solution)/shard_map/ppermute | solution.py:283
  120.2 1.2 collective-permute-start.33
  127.8 1.3 collective-permute-start.38
  129.0 4.9 %collective-permute-start.41 = (f32[8,256]{1,0:T(8,128)S(1)}, f32[8,256]{1,0:T(8,128)S(1)}, u32[]{:S(2)}, u32[]{:S(2)}) collective-permute-start(f32[8,256]{1,0:T(8,128)S(1)} %fusion.2), channel_id=1, source_target_pairs={{0,96},{1,33},{32,64},{33,1},{64,32},{65,97},{96,0},{97,65},{2,98}... | collective-permute-start | bytes 24584 | tf_op jit(solution)/shard_map/ppermute | solution.py:52
  132.0 5.2 %collective-permute-start.40 = (f32[8,256]{1,0:T(8,128)S(1)}, f32[8,256]{1,0:T(8,128)S(1)}, u32[]{:S(2)}, u32[]{:S(2)}) collective-permute-start(f32[8,256]{1,0:T(8,128)S(1)} %fusion.2), channel_id=1, source_target_pairs={{0,64},{1,65},{32,96},{33,97},{64,0},{65,1},{96,32},{97,33},{2,66}... | collective-permute-start | bytes 24584 | tf_op jit(solution)/shard_map/ppermute | solution.py:52
  132.6 4.5 %collective-permute-start.39 = (f32[8,256]{1,0:T(8,128)S(1)}, f32[8,256]{1,0:T(8,128)S(1)}, u32[]{:S(2)}, u32[]{:S(2)}) collective-permute-start(f32[8,256]{1,0:T(8,128)S(1)} %fusion.2), channel_id=1, source_target_pairs={{0,32},{1,97},{32,0},{33,65},{64,96},{65,33},{96,64},{97,1},{2,34}... | collective-permute-start | bytes 24584 | tf_op jit(solution)/shard_map/ppermute | solution.py:52
  133.2 7.7 %collective-permute-start.22 = (bf16[256,256]{1,0:T(8,128)(2,1)S(1)}, bf16[256,256]{1,0:T(8,128)(2,1)S(1)}, u32[]{:S(2)}, u32[]{:S(2)}) collective-permute-start(bf16[256,256]{1,0:T(8,128)(2,1)S(1)} %get-tuple-element.88), channel_id=1, source_target_pairs={{0,1},{1,0},{2,3},{3,2},{4,5},{5,4},{6,7},{7,6},{8,9},{9,8},{10,11... | collective-permute-start | bytes 393224 | tf_op jit(solution)/shard_map/ppermute | solution.py:283
  133.2 7.7 %collective-permute-start.37 = (bf16[256,256]{1,0:T(8,128)(2,1)S(1)}, bf16[256,256]{1,0:T(8,128)(2,1)S(1)}, u32[]{:S(2)}, u32[]{:S(2)}) collective-permute-start(bf16[256,256]{1,0:T(8,128)(2,1)S(1)} %get-tuple-element.108), channel_id=1, source_target_pairs={{0,1},{1,0},{2,3},{3,2},{4,5},{5,4},{6,7},{7,6},{8,9},{9,8},{10,11... | collective-permute-start | bytes 393224 | tf_op jit(solution)/shard_map/ppermute | solution.py:283
  137.2 3.7 %collective-permute-start.42 = (f32[8,256]{1,0:T(8,128)S(1)}, f32[8,256]{1,0:T(8,128)S(1)}, u32[]{:S(2)}, u32[]{:S(2)}) collective-permute-start(f32[8,256]{1,0:T(8,128)S(1)} %add_add_fusion), channel_id=1, source_target_pairs={{0,128},{128,0},{1,129},{129,1},{2,130},{130,2},{3,131},{131,3},{4... | collective-permute-start | bytes 24584 | tf_op jit(solution)/shard_map/ppermute | solution.py:279
